TPU v7x, 32 devices: a whole 2x2x4 slice. The times are simulated.
32 devices in a mesh: section: 2 (over core), batch: 16 (over z, y, x).
Axes of the slice: x: 2, y: 2, z: 4, core: 2. Of those that a mesh axis runs over, the one named last changes fastest.
Arguments:
- layer_input: bfloat16 [4096, 768], P('batch'), may hold values from -6 to 6
- seq_lengths: int32 [32], P('batch'), may hold values from 64 to 128, as said below
- cotangent: bfloat16 [4096, 768], P('batch'), may hold values from -6 to 6
- project_weight: bfloat16 [2, 768, 2304], P('section'), may hold values from -0.4375 to 0.4375
- project_bias: float32 [2, 1536], P('section'), may hold values from -3 to 3
- conv_kernel: float32 [2, 12, 33], P('section'), may hold values from -0.6 to 0.6
- output_weight: bfloat16 [2, 768, 768], P('section'), may hold values from -0.625 to 0.625
- output_bias: float32 [2, 768], P('section'), may hold values from -3 to 3
- attn_gain: float32 [2, 768], P('section'), may hold values from 0.5 to 1.5
- attn_shift: float32 [2, 768], P('section'), may hold values from -3 to 3
- expand_weight: bfloat16 [2, 768, 3072], P('section'), may hold values from -0.21875 to 0.21875
- expand_bias: float32 [2, 3072], P('section'), may hold values from -3 to 3
- reduce_weight: bfloat16 [2, 3072, 768], P('section'), may hold values from -0.109375 to 0.109375
- reduce_bias: float32 [2, 768], P('section'), may hold values from -3 to 3
- final_gain: float32 [2, 768], P('section'), may hold values from 0.5 to 1.5
- final_shift: float32 [2, 768], P('section'), may hold values from -3 to 3
Outputs:
- activations: bfloat16 [2, 4096, 768], P('section', 'batch')
- input_grads: bfloat16 [2, 4096, 768], P('section', 'batch')
- grad_project_weight: float32 [2, 768, 2304], P('section', 'batch')
- grad_project_bias: float32 [2, 1536], P('section', 'batch')
- grad_conv_kernel: float32 [2, 12, 33], P('section')
- grad_output_weight: float32 [2, 768, 768], P('section', 'batch')
- grad_output_bias: float32 [2, 768], P('section', 'batch')
- grad_attn_gain: float32 [2, 768], P('section', 'batch')
- grad_attn_shift: float32 [2, 768], P('section', 'batch')
- grad_expand_weight: float32 [2, 768, 3072], P('section', 'batch')
- grad_expand_bias: float32 [2, 3072], P('section', 'batch')
- grad_reduce_weight: float32 [2, 3072, 768], P('section', 'batch')
- grad_reduce_bias: float32 [2, 768], P('section', 'batch')
- grad_final_gain: float32 [2, 768], P('section', 'batch')
- grad_final_shift: float32 [2, 768], P('section', 'batch')
- proxies: float32 [2, 6], P('section')
Inputs may be any that keep to these rules, and one draw needn't show every extreme that they name: `seq_lengths`: each slot holds one sequence whose length is a multiple of 64; rows at and past the length are padding; slot 0 holds 128 tokens.
All inputs are finite; a program needn't handle non-finite values.
Results may differ from a plain program's by a relative error of at most 0.04.
Values may be sent and summed in bfloat16 or wider, within the bound.
A program may use at most 320 MiB of HBM per device.

v0:
```python
import jax
import jax.numpy as jnp
from jax import lax
from jax.sharding import PartitionSpec as P

LANDMARKS = 64
NEWTON = 6


MAXIMAL_PRECISION = lax.Precision.HIGHEST
NORM_EPSILON = 1e-05


def shifted(shard, axis, by):
    devices = lax.axis_size(axis)
    pairs = [(i, i + by) for i in range(devices) if 0 <= i + by < devices]
    return lax.ppermute(shard, axis, pairs)


def layer_norm(values, gain_vec, shift_vec):
    center = values - jnp.mean(values, axis=-1, keepdims=True)
    spread = jnp.mean(center * center, axis=-1, keepdims=True)
    return center * lax.rsqrt(spread + NORM_EPSILON) * gain_vec + shift_vec


def gelu_exact(values):
    return jax.nn.gelu(values, approximate=False)


def newton_inverse(kernel):
    landmark_count = kernel.shape[-1]
    identity = jnp.eye(landmark_count, dtype=jnp.float32)
    frobenius = jnp.sum(kernel * kernel, axis=(1, 2), keepdims=True)
    pseudo_inverse = jnp.swapaxes(kernel, 1, 2) / frobenius
    errors = []
    for newton_step in range(NEWTON):
        product = jnp.matmul(kernel, pseudo_inverse, precision=MAXIMAL_PRECISION)
        factor = 7.0 * identity - product
        factor = 15.0 * identity - jnp.matmul(product, factor, precision=MAXIMAL_PRECISION)
        factor = 13.0 * identity - jnp.matmul(product, factor, precision=MAXIMAL_PRECISION)
        pseudo_inverse = 0.25 * jnp.matmul(pseudo_inverse, factor, precision=MAXIMAL_PRECISION)
        residue = identity - jnp.matmul(kernel, pseudo_inverse, precision=MAXIMAL_PRECISION)
        errors.append(jnp.sum(residue * residue))
    return (pseudo_inverse, jnp.stack(errors))


def attention(qkv_rows, kernel_taps, length):
    slot_rows = qkv_rows.shape[0]
    head_count = kernel_taps.shape[0]
    model_width = qkv_rows.shape[1] // 3
    head_size = model_width // head_count
    positions = jnp.arange(slot_rows, dtype=jnp.int32)
    valid_rows = (positions < length).astype(jnp.float32)[:, None]
    score_scale = head_size ** (-0.25)
    queries = (qkv_rows[:, :model_width] * valid_rows * score_scale).reshape(
        slot_rows, head_count, head_size
    )
    keys_all = (qkv_rows[:, model_width : 2 * model_width] * valid_rows * score_scale).reshape(
        slot_rows, head_count, head_size
    )
    values_all = (qkv_rows[:, 2 * model_width :] * valid_rows).reshape(
        slot_rows, head_count, head_size
    )
    segment = length // LANDMARKS
    member = positions[None, :] // segment == jnp.arange(LANDMARKS, dtype=jnp.int32)[:, None]
    member = member & (positions[None, :] < length)
    pooling = member.astype(jnp.float32) / segment.astype(jnp.float32)
    landmark_queries = jnp.einsum("lr,rhd->hld", pooling, queries, precision=MAXIMAL_PRECISION)
    landmark_keys = jnp.einsum("lr,rhd->hld", pooling, keys_all, precision=MAXIMAL_PRECISION)
    kernel_first = jax.nn.softmax(
        jnp.einsum("rhd,hld->hrl", queries, landmark_keys, precision=MAXIMAL_PRECISION), axis=-1
    )
    middle_kernel = jax.nn.softmax(
        jnp.einsum("krg,kug->kru", landmark_queries, landmark_keys, precision=MAXIMAL_PRECISION),
        axis=-1,
    )
    score_last = jnp.einsum("hld,rhd->hlr", landmark_queries, keys_all, precision=MAXIMAL_PRECISION)
    score_last = jnp.where(valid_rows[:, 0][None, None, :] > 0, score_last, -1e30)
    kernel_last = jax.nn.softmax(score_last, axis=-1)
    pseudo_inverse, errors = newton_inverse(middle_kernel)
    landmark_digest = jnp.einsum(
        "hlr,rhd->hld", kernel_last, values_all, precision=MAXIMAL_PRECISION
    )
    blended_values = jnp.einsum(
        "pwc,pce->pwe", pseudo_inverse, landmark_digest, precision=MAXIMAL_PRECISION
    )
    attended = jnp.einsum("hrl,hld->rhd", kernel_first, blended_values, precision=MAXIMAL_PRECISION)
    half_width = (kernel_taps.shape[1] - 1) // 2
    padded = jnp.pad(values_all, ((half_width, half_width), (0, 0), (0, 0)))
    for tap_index in range(kernel_taps.shape[1]):
        attended = (
            attended
            + kernel_taps[:, tap_index][None, :, None] * padded[tap_index : tap_index + slot_rows]
        )
    return (attended.reshape(slot_rows, model_width), errors)


def forward_layer(layer_rows, length, params):
    (
        weight_qkv,
        bias_full,
        kernel_taps,
        weight_output,
        bias_output,
        gain_first,
        shift_first,
        weight_expand,
        bias_expand,
        weight_reduce,
        bias_reduce,
        gain_last,
        shift_last,
    ) = params
    slot_rows = layer_rows.shape[0]
    hidden = layer_rows.astype(jnp.float32)
    qkv_rows = jnp.dot(layer_rows, weight_qkv, preferred_element_type=jnp.float32) + bias_full

    def attend_local(qkv_values, taps_values):
        return attention(qkv_values, taps_values, length)

    attended, attend_back, errors = jax.vjp(attend_local, qkv_rows, kernel_taps, has_aux=True)
    attended_low = attended.astype(jnp.bfloat16)
    projected = (
        jnp.dot(attended_low, weight_output, preferred_element_type=jnp.float32) + bias_output
    )
    first, first_back = jax.vjp(layer_norm, hidden + projected, gain_first, shift_first)
    first_low = first.astype(jnp.bfloat16)
    up_proj = jnp.dot(first_low, weight_expand, preferred_element_type=jnp.float32) + bias_expand
    activated, gelu_back = jax.vjp(gelu_exact, up_proj)
    activated_low = activated.astype(jnp.bfloat16)
    down_proj = (
        jnp.dot(activated_low, weight_reduce, preferred_element_type=jnp.float32) + bias_reduce
    )
    normed, last_back = jax.vjp(layer_norm, first + down_proj, gain_last, shift_last)
    valid_rows = (jnp.arange(slot_rows, dtype=jnp.int32) < length).astype(jnp.float32)[:, None]
    kept = (
        layer_rows,
        attend_back,
        attended_low,
        first_back,
        first_low,
        gelu_back,
        activated_low,
        last_back,
        valid_rows,
    )
    return (normed * valid_rows, errors, kept)


def backward_layer(grad_rows, kept, params):
    (
        weight_qkv,
        bias_full,
        kernel_taps,
        weight_output,
        bias_output,
        gain_first,
        shift_first,
        weight_expand,
        bias_expand,
        weight_reduce,
        bias_reduce,
        gain_last,
        shift_last,
    ) = params
    (
        layer_rows,
        attend_back,
        attended_low,
        first_back,
        first_low,
        gelu_back,
        activated_low,
        last_back,
        valid_rows,
    ) = kept
    model_width = layer_rows.shape[1]
    grad_second, grad_gain_last, grad_shift_last = last_back(
        grad_rows.astype(jnp.float32) * valid_rows
    )
    grad_down = grad_second.astype(jnp.bfloat16)
    grad_weight_reduce = jnp.dot(activated_low.T, grad_down, preferred_element_type=jnp.float32)
    grad_bias_reduce = jnp.sum(grad_down.astype(jnp.float32), axis=0)
    grad_activated = jnp.dot(grad_down, weight_reduce.T, preferred_element_type=jnp.float32)
    grad_up = gelu_back(grad_activated)[0].astype(jnp.bfloat16)
    grad_weight_expand = jnp.dot(first_low.T, grad_up, preferred_element_type=jnp.float32)
    grad_bias_expand = jnp.sum(grad_up.astype(jnp.float32), axis=0)
    grad_first = grad_second + jnp.dot(grad_up, weight_expand.T, preferred_element_type=jnp.float32)
    grad_residual, grad_gain_first, grad_shift_first = first_back(grad_first)
    grad_projected = grad_residual.astype(jnp.bfloat16)
    grad_weight_output = jnp.dot(attended_low.T, grad_projected, preferred_element_type=jnp.float32)
    grad_bias_output = jnp.sum(grad_projected.astype(jnp.float32), axis=0)
    grad_attended = jnp.dot(grad_projected, weight_output.T, preferred_element_type=jnp.float32)
    grad_qkv, grad_taps = attend_back(grad_attended)
    grad_qkv_low = grad_qkv.astype(jnp.bfloat16)
    grad_weight_qkv = jnp.dot(layer_rows.T, grad_qkv_low, preferred_element_type=jnp.float32)
    column_sums = jnp.sum(grad_qkv_low.astype(jnp.float32), axis=0)
    grad_bias_qv = jnp.concatenate([column_sums[:model_width], column_sums[2 * model_width :]])
    grad_input = grad_residual + jnp.dot(
        grad_qkv_low, weight_qkv.T, preferred_element_type=jnp.float32
    )
    matrices = (
        grad_weight_qkv,
        grad_bias_qv,
        grad_weight_output,
        grad_bias_output,
        grad_gain_first,
        grad_shift_first,
        grad_weight_expand,
        grad_bias_expand,
        grad_weight_reduce,
        grad_bias_reduce,
        grad_gain_last,
        grad_shift_last,
    )
    return (matrices, grad_taps, grad_input)


def body(
    layer_input,
    seq_lengths,
    cotangent,
    project_weight,
    project_bias,
    conv_kernel,
    output_weight,
    output_bias,
    attn_gain,
    attn_shift,
    expand_weight,
    expand_bias,
    reduce_weight,
    reduce_bias,
    final_gain,
    final_shift,
):
    section_index = lax.axis_index("section")
    first_section = section_index == 0
    total_rows, model_width = layer_input.shape
    micro_count = seq_lengths.shape[0]
    slot_rows = total_rows // micro_count
    bias_pair = project_bias[0]
    bias_full = jnp.concatenate(
        [bias_pair[:model_width], jnp.zeros((model_width,), jnp.float32), bias_pair[model_width:]]
    )
    params = (
        project_weight[0],
        bias_full,
        conv_kernel[0],
        output_weight[0],
        output_bias[0],
        attn_gain[0],
        attn_shift[0],
        expand_weight[0],
        expand_bias[0],
        reduce_weight[0],
        reduce_bias[0],
        final_gain[0],
        final_shift[0],
    )
    empty_rows = jnp.zeros((slot_rows, model_width), jnp.bfloat16)
    received = empty_rows
    error_total = jnp.zeros((NEWTON,), jnp.float32)
    layer_outputs = []
    saved_list = []
    for turn_index in range(micro_count + 1):
        if turn_index < micro_count:
            own_rows = layer_input[turn_index * slot_rows : (turn_index + 1) * slot_rows]
        else:
            own_rows = empty_rows
        layer_rows = jnp.where(first_section, own_rows, received)
        length = jnp.where(
            first_section,
            seq_lengths[min(turn_index, micro_count - 1)],
            seq_lengths[max(turn_index - 1, 0)],
        )
        normed, errors, kept = forward_layer(layer_rows, length, params)
        live_turn = jnp.where(first_section, turn_index < micro_count, turn_index >= 1)
        error_total = error_total + jnp.where(live_turn, errors, 0.0)
        normed_low = normed.astype(jnp.bfloat16)
        layer_outputs.append(normed_low)
        saved_list.append(kept)
        if turn_index < micro_count:
            received = shifted(normed_low, "section", 1)
    activations = jnp.concatenate(
        [
            jnp.where(first_section, layer_outputs[micro_index], layer_outputs[micro_index + 1])
            for micro_index in range(micro_count)
        ],
        axis=0,
    )
    back_received = empty_rows
    grad_outputs = []
    totals = None
    shares = None
    taps_total = jnp.zeros_like(conv_kernel[0])
    for turn_index in range(micro_count + 1):
        micro_index = micro_count - 1 - turn_index
        if turn_index < micro_count:
            own_grads = cotangent[micro_index * slot_rows : (micro_index + 1) * slot_rows]
        else:
            own_grads = empty_rows
        grad_rows = jnp.where(first_section, back_received, own_grads)
        matrices, grad_taps, grad_input = backward_layer(
            grad_rows, saved_list[micro_count - turn_index], params
        )
        grad_low = grad_input.astype(jnp.bfloat16)
        grad_outputs.append(grad_low)
        taps_total = taps_total + grad_taps
        if turn_index < micro_count:
            back_received = shifted(grad_low, "section", -1)
        totals = (
            matrices
            if totals is None
            else tuple((total + matrix for total, matrix in zip(totals, matrices)))
        )
    shares = lax.psum_scatter(totals, "batch", scatter_dimension=0, tiled=True)
    input_grads = jnp.concatenate(
        [
            jnp.where(
                first_section,
                grad_outputs[micro_count - micro_index],
                grad_outputs[micro_count - 1 - micro_index],
            )
            for micro_index in range(micro_count)
        ],
        axis=0,
    )
    taps_sum, proxies = lax.psum((taps_total, error_total), "batch")
    return (
        activations[None],
        input_grads[None],
        shares[0][None],
        shares[1][None],
        taps_sum[None],
        shares[2][None],
        shares[3][None],
        shares[4][None],
        shares[5][None],
        shares[6][None],
        shares[7][None],
        shares[8][None],
        shares[9][None],
        shares[10][None],
        shares[11][None],
        proxies[None],
    )


def solution(mesh):
    return jax.shard_map(
        body,
        mesh=mesh,
        in_specs=(
            P("batch", None),
            P("batch"),
            P("batch", None),
            P("section", None, None),
            P("section", None),
            P("section", None, None),
            P("section", None, None),
            P("section", None),
            P("section", None),
            P("section", None),
            P("section", None, None),
            P("section", None),
            P("section", None, None),
            P("section", None),
            P("section", None),
            P("section", None),
        ),
        out_specs=(
            P("section", "batch", None),
            P("section", "batch", None),
            P("section", "batch", None),
            P("section", "batch"),
            P("section", None, None),
            P("section", "batch", None),
            P("section", "batch"),
            P("section", "batch"),
            P("section", "batch"),
            P("section", "batch", None),
            P("section", "batch"),
            P("section", "batch", None),
            P("section", "batch"),
            P("section", "batch"),
            P("section", "batch"),
            P("section", None),
        ),
        check_vma=False,
    )
```

profile of v0, /device:TPU:0, one launch (start us, length us, event | category | flops | bytes accessed | tf_op | source)
XLA Modules:
  0.0 1123.0 jit_solution(5415448704389152870)
XLA Ops:
  68.8 6.1 fusion.282
  75.8 7.4 multiply_convert_fusion.2
  147.6 5.5 fusion.281
  154.0 7.4 multiply_convert_fusion.1
  207.8 5.9 fusion.280
  214.5 4.9 multiply_convert_fusion
  294.9 10.1 pad_add_fusion.2
  325.4 3.4 multiply_reduce_fusion.85
  367.6 3.4 broadcast_multiply_fusion.9
  392.2 9.7 pad_add_fusion.1
  410.9 4.1 fusion.662
  426.8 3.4 multiply_reduce_fusion.52
  494.9 5.8 pad_add_fusion
  510.6 4.0 add_add_fusion.2
  520.0 5.8 add_add_fusion.1
  530.3 5.0 add_add_fusion
  544.9 4.5 stack.83
  549.3 4.4 stack.76
  553.7 4.3 stack.69
  563.4 7.4 multiply_reduce_fusion.119
  581.7 81.0 %all-reduce.218 = (f32[1536]{0:T(1024)}, f32[1,12,33]{1,2,0:T(8,128)}, f32[768]{0:T(1024)}, f32[768]{0:T(1024)}, f32[768]{0:T(1024)}, /*index=5*/f32[3072]{0:T(1...) all-reduce(f32[1536]{0:T(1024)} %fusion.522, ...), channel_id=3, replica_groups=mesh['section'=2,'batch'=16] {'batch'}, use_global_device_ids=true, to_apply=%region_61.62.clone | all-reduce | flops 9618 | bytes 76944
  677.5 85.8 %reduce-scatter.5.cloned.1.call-done = f32[48,2304]{1,0:T(8,128)} async-done(((f32[768,2304]{1,0:T(8,128)}), f32[48,2304]{1,0:T(8,128)}) %reduce-scatter.5.cloned.1.call-update) | async-done | bytes 442384 | tf_op jit(solution)/shard_map/reduce_scatter | solution.py:317
  763.3 176.9 %reduce-scatter.9.cloned.1.call-done = f32[48,3072]{1,0:T(8,128)} async-done(((f32[768,3072]{1,0:T(8,128)}), f32[48,3072]{1,0:T(8,128)}) %reduce-scatter.9.cloned.1.call-update) | async-done | bytes 589840 | tf_op jit(solution)/shard_map/reduce_scatter | solution.py:317
  940.2 176.0 %reduce-scatter.11.cloned.1.call-done = f32[192,768]{1,0:T(8,128)} async-done(((f32[3072,768]{1,0:T(8,128)}), f32[192,768]{1,0:T(8,128)}) %reduce-scatter.11.cloned.1.call-update) | async-done | bytes 589840 | tf_op jit(solution)/shard_map/reduce_scatter | solution.py:317
  (1870 shorter events, 456.9 us)
Async XLA Ops:
  7.2 670.3 %reduce-scatter.7.cloned.1.call-start = ((), (), s32[]{:S(2)}) async-start(), calls=%async_computation.5 | async-start | bytes 2506752 | tf_op jit(solution)/shard_map/reduce_scatter | solution.py:317
  35.5 65.2 %copy-start.305 = (f32[12,64]{1,0:T(8,128)}, f32[12,64]{1,0:T(8,128)S(1)}, u32[]{:S(2)}) copy-start(f32[12,64]{1,0:T(8,128)S(1)} %get-tuple-element.402) | copy-start | bytes 9220
  86.6 19.7 %collective-permute-start = (bf16[128,768]{1,0:T(8,128)(2,1)}, bf16[128,768]{1,0:T(8,128)(2,1)}, u32[]{:S(2)}, u32[]{:S(2)}) collective-permute-start(bf16[128,768]{1,0:T(8,128)(2,1)} %multiply_convert_fusion.5), channel_id=1, source_target_pairs={{0,16},{1,17},{2,18},{3,19},{4,20},{5,21},{6,22},{7,23},{8,24},{9,... | collective-permute-start | bytes 589832 | tf_op jit(solution)/shard_map/ppermute | solution.py:17
  164.6 2.3 collective-permute-start.1
  179.0 110.7 %copy-start.301 = (f32[12,64]{1,0:T(8,128)}, f32[12,64]{1,0:T(8,128)S(1)}, u32[]{:S(2)}) copy-start(f32[12,64]{1,0:T(8,128)S(1)} %get-tuple-element.424) | copy-start | bytes 9220
  204.7 63.9 %copy-start.149 = (f32[12,64,128]{2,1,0:T(8,128)}, f32[12,64,128]{2,1,0:T(8,128)S(1)}, u32[]{:S(2)}) copy-start(f32[12,64,128]{2,1,0:T(8,128)S(1)} %get-tuple-element.427) | copy-start | bytes 1179652
  204.7 63.9 %copy-start.345 = (f32[12,64]{1,0:T(8,128)}, f32[12,64]{1,0:T(8,128)S(1)}, u32[]{:S(2)}) copy-start(f32[12,64]{1,0:T(8,128)S(1)} %get-tuple-element.426) | copy-start | bytes 9220
  205.1 63.6 %copy-start.364 = (f32[12,64]{1,0:T(8,128)}, f32[12,64]{1,0:T(8,128)S(1)}, u32[]{:S(2)}) copy-start(f32[12,64]{1,0:T(8,128)S(1)} %fusion.363) | copy-start | bytes 9220
  232.6 50.4 %copy-start.96 = (f32[128,12,64]{0,2,1:T(8,128)}, f32[128,12,64]{0,2,1:T(8,128)S(1)}, u32[]{:S(2)}) copy-start(f32[128,12,64]{0,2,1:T(8,128)S(1)} %get-tuple-element.444) | copy-start | bytes 1179652
  233.9 32.8 %copy-start.257 = (f32[12,64,64]{2,1,0:T(8,128)}, f32[12,64,64]{2,1,0:T(8,128)S(1)}, u32[]{:S(2)}) copy-start(f32[12,64,64]{2,1,0:T(8,128)S(1)} %fusion.620) | copy-start | bytes 589828
  313.5 3.6 collective-permute-start.2
  328.8 51.3 %copy-start.98 = (f32[128,12,64]{0,2,1:T(8,128)}, f32[128,12,64]{0,2,1:T(8,128)S(1)}, u32[]{:S(2)}) copy-start(f32[128,12,64]{0,2,1:T(8,128)S(1)} %get-tuple-element.454) | copy-start | bytes 1179652
  330.5 32.8 %copy-start.259 = (f32[12,64,64]{2,1,0:T(8,128)}, f32[12,64,64]{2,1,0:T(8,128)S(1)}, u32[]{:S(2)}) copy-start(f32[12,64,64]{2,1,0:T(8,128)S(1)} %fusion.634) | copy-start | bytes 589828
  415.1 3.5 collective-permute-start.3
  431.9 32.7 %copy-start.255 = (f32[12,64,64]{2,1,0:T(8,128)}, f32[12,64,64]{2,1,0:T(8,128)S(1)}, u32[]{:S(2)}) copy-start(f32[12,64,64]{2,1,0:T(8,128)S(1)} %fusion.648) | copy-start | bytes 589828
  476.4 286.9 %reduce-scatter.5.cloned.1.call-start = ((), (), s32[]{:S(2)}) async-start(), calls=%async_computation.4 | async-start | bytes 7520256 | tf_op jit(solution)/shard_map/reduce_scatter | solution.py:317
  514.7 425.5 %reduce-scatter.9.cloned.1.call-start = ((), (), s32[]{:S(2)}) async-start(), calls=%async_computation.6 | async-start | bytes 10027008 | tf_op jit(solution)/shard_map/reduce_scatter | solution.py:317
  525.9 590.3 %reduce-scatter.11.cloned.1.call-start = ((), (), s32[]{:S(2)}) async-start(), calls=%async_computation.7 | async-start | bytes 10027008 | tf_op jit(solution)/shard_map/reduce_scatter | solution.py:317
  561.5 19.6 %copy-start.389 = (f32[768]{0:T(1024)S(1)}, f32[768]{0:T(1024)}, u32[]{:S(2)}) copy-start(f32[768]{0:T(1024)} %get-tuple-element.175) | copy-start | bytes 9220
  561.5 19.6 %copy-start.393 = (f32[768]{0:T(1024)S(1)}, f32[768]{0:T(1024)}, u32[]{:S(2)}) copy-start(f32[768]{0:T(1024)} %get-tuple-element.179) | copy-start | bytes 9220
  561.5 19.6 %copy-start.397 = (f32[768]{0:T(1024)S(1)}, f32[768]{0:T(1024)}, u32[]{:S(2)}) copy-start(f32[768]{0:T(1024)} %get-tuple-element.180) | copy-start | bytes 9220
  561.5 20.2 %copy-start.423 = (f32[3072]{0:T(1024)S(1)}, f32[3072]{0:T(1024)}, u32[]{:S(2)}) copy-start(f32[3072]{0:T(1024)} %get-tuple-element.469) | copy-start | bytes 36868
  561.5 20.2 %copy-start.424 = (f32[3072]{0:T(1024)S(1)}, f32[3072]{0:T(1024)}, u32[]{:S(2)}) copy-start(f32[3072]{0:T(1024)} %get-tuple-element.471) | copy-start | bytes 36868
  561.5 20.1 %copy-start.425 = (f32[3072]{0:T(1024)S(1)}, f32[3072]{0:T(1024)}, u32[]{:S(2)}) copy-start(f32[3072]{0:T(1024)} %get-tuple-element.467) | copy-start | bytes 36868
  (663 other events, 2697.0 us)
Sparse Core Ops, SparseCore 0:
  476.5 129.6 reduce-scatter.6
  613.0 150.2 reduce-scatter.4
  770.5 169.6 reduce-scatter.8
  946.3 169.8 reduce-scatter.10
where the time goes:
time: 1130 us; the launch traced here: 1120 us
  waiting for transfers between devices  441 us (39%)
  matrix products  356 us (32%)
  other arithmetic  122 us (11%)
  blocking collectives  81 us (7%)
  local copies, waits for them, and re-layouts  80.9 us (7%)
  between operations  33.9 us (3%)
    reduce_scatter x4, waiting for transfers between devices, body(): shares = lax.psum_scatter(totals, 'batch', scatter_dimension=0, tiled=True)  439 us
    unnamed x1, blocking collectives  81 us
    dot_general x108, matrix products, newton_inverse(): jnp.matmul(product, factor, precision=MAXIMAL_PRECISION)  76.6 us
    dot_general x54, matrix products, newton_inverse(): jnp.matmul(pseudo_inverse, factor, precision=MAXIMAL_PRECISION)  42.2 us
    dot_general x54, matrix products, newton_inverse(): product = jnp.matmul(kernel, pseudo_inverse, precision=MAXIMAL_PRECISION)  42.1 us
    add_any x3, other arithmetic, attention(): padded[tap_index:tap_index + slot_rows]  25.5 us
  transfers between devices with their start and end apart: 8, of which 6 were waited for; matrix products, arithmetic and copies ran while one was open for 11% of the time, Pallas kernels for 0%

commit v1 on v0

v1 whole, which is shorter than its diff:
```python
import functools
import math

import jax
import jax.numpy as jnp
from jax import lax
from jax.experimental import pallas as pl
from jax.experimental.pallas import tpu as pltpu
from jax.sharding import PartitionSpec as P

F32 = jnp.float32
BF16 = jnp.bfloat16
NEWTON = 6
LM = 64
PAIR = 128
EPS = 1e-05
MESH = pl.DeviceIdType.MESH


def nn(a, b):
    return lax.dot_general(a, b, (((1,), (0,)), ((), ())), preferred_element_type=F32)


def nt(a, b):
    return lax.dot_general(a, b, (((1,), (1,)), ((), ())), preferred_element_type=F32)


def tn(a, b):
    return lax.dot_general(a, b, (((0,), (0,)), ((), ())), preferred_element_type=F32)


def split(x):
    high = x.astype(BF16)
    return high, (x - high.astype(F32)).astype(BF16)


def cat(parts, axis):
    return jnp.concatenate(parts, axis=axis)


def lane_is_first(rows, width=PAIR):
    return lax.broadcasted_iota(jnp.int32, (rows, width), 1) < width // 2


def spread(y):
    rows = y.shape[0]
    keep = lane_is_first(rows).astype(F32).astype(y.dtype)
    return cat([y * keep, y * (1 - keep)], 0)


def pick(x):
    rows = x.shape[0] // 2
    return jnp.where(lane_is_first(rows), x[:rows], x[rows:])


def nn3(xs, ys):
    (xh, xl), (yh, yl) = xs, ys
    dh, dl = spread(yh), spread(yl)
    return nn(cat([xh, xl], 1), cat([dh, dh], 0)) + nn(xh, dl)


def nt3(xs, ds):
    (xh, xl), (dh, dl) = xs, ds
    return nt(cat([xh, xl], 1), cat([dh, dh], 1)) + nt(xh, dl)


def half_sums(x, ones):
    high, low = split(x)
    return nn(high, ones) + nn(low, ones)


def block_ones():
    row = lax.broadcasted_iota(jnp.int32, (PAIR, PAIR), 0) < LM
    col = lax.broadcasted_iota(jnp.int32, (PAIR, PAIR), 1) < LM
    return (row == col).astype(F32).astype(BF16)


def pair_softmax(scores, ones):
    first = lane_is_first(scores.shape[0])
    top_a = jnp.max(jnp.where(first, scores, -jnp.inf), axis=1, keepdims=True)
    top_b = jnp.max(jnp.where(first, -jnp.inf, scores), axis=1, keepdims=True)
    e = jnp.exp(scores - jnp.where(first, top_a, top_b))
    return e / half_sums(e, ones)


def pair_transpose(x):
    t = x.T
    return cat([t[:LM], t[LM:]], 1)


def pair_eye():
    row = lax.broadcasted_iota(jnp.int32, (LM, PAIR), 0)
    col = lax.broadcasted_iota(jnp.int32, (LM, PAIR), 1)
    return (row == col % LM).astype(F32)


def pool_matrix(length, rows):
    landmark = lax.broadcasted_iota(jnp.int32, (LM, rows), 0)
    row = lax.broadcasted_iota(jnp.int32, (LM, rows), 1)
    segment = length // LM
    inside = (row >= landmark * segment) & (row < (landmark + 1) * segment)
    weight = 1.0 / jnp.full((LM, rows), segment, jnp.int32).astype(F32)
    return jnp.where(inside, weight, 0.0).astype(BF16)


def toeplitz(taps_row, rows, taps):
    half = taps // 2
    wide = jnp.broadcast_to(taps_row, (rows, rows))
    wide = pltpu.roll(wide, rows - half, 1, stride=1, stride_axis=0)
    row = lax.broadcasted_iota(jnp.int32, (rows, rows), 0)
    col = lax.broadcasted_iota(jnp.int32, (rows, rows), 1)
    near = (col - row <= half) & (row - col <= half)
    return jnp.where(near, wide, 0.0)


def attention_forward(
    sel_ref, x_ref, bias_ref, taps_ref, own_ref, other_ref,
    att_ref, qkv_ref, lm_ref, a1_ref, a2_ref, a3_ref, t_ref, newton_ref, db_ref, err_ref,
    w_ref, sem, *, taps):
    rows, width = x_ref.shape
    pairs = width // PAIR
    length = sel_ref[1]

    def part(i, source):
        cols = pl.ds(i * width, width)
        return pltpu.make_async_copy(source.at[:, cols], w_ref.at[:, cols], sem.at[i])

    @pl.when(sel_ref[0] == 1)
    def _():
        for i in range(3):
            part(i, own_ref).start()

    @pl.when(sel_ref[0] == 0)
    def _():
        for i in range(3):
            part(i, other_ref).start()

    ones = block_ones()
    pool = pool_matrix(length, rows)
    eye = pair_eye()
    sl = [pl.ds(p * PAIR, PAIR) for p in range(pairs)]
    for p in range(pairs):
        for j in range(2):
            t_ref[p, :, j * rows:(j + 1) * rows] = toeplitz(
                taps_ref[2 * p + j:2 * p + j + 1, :], rows, taps)
    valid = (lax.broadcasted_iota(jnp.int32, (rows, width), 0) < length).astype(F32)
    scale = LM ** (-0.25)
    x = x_ref[...]
    qkv = []
    for i in range(3):
        part(i, own_ref).wait()
        y = nn(x, w_ref[:, i * width:(i + 1) * width]) + bias_ref[i:i + 1, :]
        qkv.append(y * valid * (scale if i < 2 else 1.0))
    q, k, v = [[m[:, p * PAIR:(p + 1) * PAIR] for p in range(pairs)] for m in qkv]
    qs = [split(m) for m in q]
    ks = [split(m) for m in k]
    vs = [split(m) for m in v]
    for i, ms in enumerate((qs, ks, vs)):
        for p in range(pairs):
            qkv_ref[i, :, sl[p]] = ms[p][0]
    qls = [split(nn(pool, h) + nn(pool, l)) for h, l in qs]
    kls = [split(nn(pool, h) + nn(pool, l)) for h, l in ks]
    for p in range(pairs):
        lm_ref[0, :, sl[p]] = qls[p][0]
        lm_ref[1, :, sl[p]] = kls[p][0]
    kld = [(spread(h), spread(l)) for h, l in kls]
    for p in range(pairs):
        a2_ref[:, sl[p]] = pair_softmax(nt3(qls[p], kld[p]), ones)
    first = lane_is_first(LM)
    for p in range(pairs):
        a = a2_ref[:, sl[p]]
        squares = jnp.sum(a * a, axis=0, keepdims=True)
        fro_a = jnp.sum(jnp.where(first[:1], squares, 0.0), axis=1, keepdims=True)
        fro_b = jnp.sum(jnp.where(first[:1], 0.0, squares), axis=1, keepdims=True)
        newton_ref[0, 0, :, sl[p]] = pair_transpose(a) / jnp.where(first[:1], fro_a, fro_b)
    for p in range(pairs):
        z = split(newton_ref[0, 0, :, sl[p]])
        newton_ref[1, 0, :, sl[p]] = eye - nn3(split(a2_ref[:, sl[p]]), z)

    def newton_step(step, carry):
        s_all, t_all = [], []
        for p in range(pairs):
            r = newton_ref[1, step, :, sl[p]]
            rs = split(r)
            s = nn3(rs, rs)
            newton_ref[2, step, :, sl[p]] = s
            s_all.append((r, rs, s))
        for p in range(pairs):
            r, rs, s = s_all[p]
            t = nn3(split(s), rs)
            newton_ref[3, step, :, sl[p]] = t
            t_all.append(eye + r + s + 0.25 * t)
        for p in range(pairs):
            zn = nn3(split(newton_ref[0, step, :, sl[p]]), split(t_all[p]))
            newton_ref[0, step + 1, :, sl[p]] = zn
            rn = eye - nn3(split(a2_ref[:, sl[p]]), split(zn))
            newton_ref[1, step + 1, :, sl[p]] = rn
            err_ref[step, :, sl[p]] = jnp.sum(rn * rn, axis=0, keepdims=True)
        return carry

    lax.fori_loop(0, NEWTON, newton_step, 0)
    for p in range(pairs):
        wide = slice(p * 2 * rows, (p + 1) * 2 * rows)
        score = nt3(qls[p], (spread(ks[p][0]), spread(ks[p][1])))
        key = lax.broadcasted_iota(jnp.int32, (LM, rows), 1)
        halves = []
        for j in range(2):
            sc = jnp.where(key < length, score[:, j * rows:(j + 1) * rows], -1e30)
            e = jnp.exp(sc - jnp.max(sc, axis=1, keepdims=True))
            halves.append(e / jnp.sum(e, axis=1, keepdims=True))
        a3 = cat(halves, 1)
        a3_ref[:, wide] = a3
        a3h, a3l = split(a3)
        vh, vl = spread(vs[p][0]), spread(vs[p][1])
        d = nn(a3h, vh) + (nn(a3l, vh) + nn(a3h, vl))
        z = split(newton_ref[0, NEWTON, :, sl[p]])
        ds = split(d)
        b = nn3(z, ds)
        bs = split(b)
        db_ref[0, :, sl[p]] = ds[0]
        db_ref[1, :, sl[p]] = bs[0]
        a1 = pair_softmax(nt3(qs[p], kld[p]), ones)
        a1_ref[:, sl[p]] = a1
        th, tl = split(t_ref[p])
        o = nn3(split(a1), bs) + nn(cat([th, tl], 1), cat([vh, vh], 0)) + nn(th, vl)
        att_ref[:, sl[p]] = o.astype(BF16)


def softmax_back(a, da, ones):
    return a * (da - half_sums(a * da, ones))


def attention_backward(
    sel_ref, do_ref, gr_ref, qkv_ref, lm_ref, a1_ref, a2_ref, a3_ref, t_ref, newton_ref, db_ref,
    own_ref, other_ref,
    dqkv_ref, gi_ref, col_ref, dtaps_ref,
    w_ref, dz_ref, dr_ref, da_ref, sem, *, taps):
    rows, width = do_ref.shape
    pairs = width // PAIR
    length = sel_ref[1]

    def part(i, source):
        return pltpu.make_async_copy(source.at[:, pl.ds(i * width, width)], w_ref.at[i], sem.at[i])

    @pl.when(sel_ref[0] == 1)
    def _():
        for i in range(3):
            part(i, own_ref).start()

    @pl.when(sel_ref[0] == 0)
    def _():
        for i in range(3):
            part(i, other_ref).start()

    ones = block_ones()
    eye = pair_eye()
    pool = pool_matrix(length, rows)
    sl = [pl.ds(p * PAIR, PAIR) for p in range(pairs)]
    doh = [do_ref[:, sl[p]].astype(BF16) for p in range(pairs)]
    ddh = []
    for p in range(pairs):
        a1 = a1_ref[:, sl[p]].astype(BF16)
        db = pick(tn(a1, doh[p]))
        dbh = db.astype(BF16)
        z = newton_ref[0, NEWTON, :, sl[p]].astype(BF16)
        dz_ref[:, sl[p]] = nt(dbh, spread(db_ref[0, :, sl[p]]))
        dr_ref[:, sl[p]] = jnp.zeros((LM, PAIR), F32)
        ddh.append(pick(tn(z, dbh)).astype(BF16))

    def newton_back(index, carry):
        step = NEWTON - 1 - index
        keep = []
        for p in range(pairs):
            z = newton_ref[0, step, :, sl[p]]
            zh, zl = split(z)
            dz = dz_ref[:, sl[p]]
            gh, gl = split(dz)
            full = tn(cat([zh, zh, zl], 0), cat([gh, gl, gh], 0))
            df = pick(full + full.T) * 0.5
            keep.append((df, (gh, gl)))
        for p in range(pairs):
            df, g = keep[p]
            r, s, t = [newton_ref[i, step, :, sl[p]] for i in (1, 2, 3)]
            dz_ref[:, sl[p]] = nn3(g, split(eye + r + s + 0.25 * t))
            dr = dr_ref[:, sl[p]]
            dt = 0.25 * df + 0.75 * dr
            rs, ss, dts, drs = split(r), split(s), split(dt), split(0.5 * dr)
            m = nn3(dts, rs) + nn3(drs, ss)
            keep[p] = (df, dts, m, rs, ss)
        for p in range(pairs):
            df, dts, m, rs, ss = keep[p]
            ds = 2.0 * df + (m + pair_transpose(m))
            m = nn3(dts, ss) + nn3(split(ds), rs)
            dr_ref[:, sl[p]] = df + 0.5 * (m + pair_transpose(m))
        return carry

    lax.fori_loop(0, NEWTON, newton_back, 0)
    first = lane_is_first(1)
    for p in range(pairs):
        a = a2_ref[:, sl[p]]
        at = pair_transpose(a)
        dz = dz_ref[:, sl[p]]
        g = nn3(split(dr_ref[:, sl[p]]), split(a))

        def halves(m):
            c = jnp.sum(m, axis=0, keepdims=True)
            ca = jnp.sum(jnp.where(first, c, 0.0), axis=1, keepdims=True)
            cb = jnp.sum(jnp.where(first, 0.0, c), axis=1, keepdims=True)
            return jnp.where(first, ca, cb)

        inv = 1.0 / halves(a * a)
        dc = halves(dz * at) - halves(g * a)
        da_ref[:, sl[p]] = inv * (pair_transpose(dz) - 2.0 * g) - (2.0 * dc * inv * inv) * a
    scale = LM ** (-0.25)
    valid = (lax.broadcasted_iota(jnp.int32, (rows, PAIR), 0) < length).astype(F32)
    half = taps // 2
    row = lax.broadcasted_iota(jnp.int32, (rows, rows), 0)
    col = lax.broadcasted_iota(jnp.int32, (rows, rows), 1)
    flip = (row + col == rows - 1).astype(F32).astype(BF16)
    near = (col + row <= rows - 1 + half) & (col + row >= rows - 1 - half)
    for p in range(pairs):
        q, k, v = [qkv_ref[i, :, sl[p]] for i in range(3)]
        ql, kl = lm_ref[0, :, sl[p]], lm_ref[1, :, sl[p]]
        kld, kd, vd = spread(kl), spread(k), spread(v)
        wide = slice(p * 2 * rows, (p + 1) * 2 * rows)
        ds2 = softmax_back(a2_ref[:, sl[p]], da_ref[:, sl[p]], ones).astype(BF16)
        a1 = a1_ref[:, sl[p]]
        da1 = nt(doh[p], spread(db_ref[1, :, sl[p]]))
        ds1 = softmax_back(a1, da1, ones).astype(BF16)
        a3 = a3_ref[:, wide]
        da3 = nt(ddh[p], vd)
        parts = []
        for j in range(2):
            a, d = a3[:, j * rows:(j + 1) * rows], da3[:, j * rows:(j + 1) * rows]
            parts.append(a * (d - jnp.sum(a * d, axis=1, keepdims=True)))
        ds3 = cat(parts, 1).astype(BF16)
        th = t_ref[p].astype(BF16)
        dv = pick(tn(cat([a3.astype(BF16), th], 0), cat([ddh[p], doh[p]], 0)))
        full = nt(spread(nn(flip, doh[p]).astype(BF16)), v)
        for j in range(2):
            m = jnp.where(near, full[j * rows:(j + 1) * rows], 0.0)
            m = pltpu.roll(m, half + 1, 1, stride=1, stride_axis=0)
            dtaps_ref[2 * p + j:2 * p + j + 1, :] = jnp.sum(m, axis=0, keepdims=True)
        dkl = pick(tn(cat([ds1, ds2], 0), cat([q, ql], 0)))
        dql = nn(cat([ds2, ds3], 1), cat([kld, kd], 0))
        dqlh, dqll = split(dql)
        dklh, dkll = split(dkl)
        dq = nn(ds1, kld) + (tn(pool, dqlh) + tn(pool, dqll))
        dk = pick(tn(ds3, ql)) + (tn(pool, dklh) + tn(pool, dkll))
        for i, m in enumerate((dq * scale, dk * scale, dv)):
            low = (m * valid).astype(BF16)
            dqkv_ref[:, pl.ds(i * width + p * PAIR, PAIR)] = low
    for i in range(3):
        col_ref[i:i + 1, :] = jnp.sum(
            dqkv_ref[:, i * width:(i + 1) * width].astype(F32), axis=0, keepdims=True)
    total = gr_ref[...]
    for i in range(3):
        part(i, own_ref).wait()
        total = total + nt(dqkv_ref[:, i * width:(i + 1) * width], w_ref[i])
    gi_ref[...] = total.astype(BF16)


def weight_copies(groups, own_refs, other_refs, buffers, sem, flag):
    def make(i, refs):
        w, rows, cols = groups[i]
        return pltpu.make_async_copy(refs[w].at[rows, cols], buffers[w].at[rows, cols], sem.at[i])

    @pl.when(flag == 1)
    def _():
        for i in range(len(groups)):
            make(i, own_refs).start()

    @pl.when(flag == 0)
    def _():
        for i in range(len(groups)):
            make(i, other_refs).start()

    return lambda i: make(i, own_refs).wait()


def erf(x):
    return lax.erf(x)


def norm_forward(values):
    center = values - jnp.mean(values, axis=1, keepdims=True)
    rstd = lax.rsqrt(jnp.mean(center * center, axis=1, keepdims=True) + EPS)
    return center * rstd, rstd


def norm_back(grad, hat, rstd):
    mean = jnp.mean(grad, axis=1, keepdims=True)
    slope = jnp.mean(grad * hat, axis=1, keepdims=True)
    return rstd * (grad - mean - hat * slope)


def post_forward(
    sel_ref, att_ref, x_ref, vec_ref, wo_own, we_own, wr_own, wo_oth, we_oth, wr_oth,
    y_ref, first_ref, act_ref, hat1_ref, hat2_ref, rstd_ref, slope_ref,
    wo_ref, we_ref, wr_ref, sem):
    rows, width = x_ref.shape
    chunks = act_ref.shape[1] // width
    every = pl.ds(0, width)
    piece = [pl.ds(c * width, width) for c in range(chunks)]
    groups = [(0, every, every)]
    for c in range(chunks):
        groups += [(1, every, piece[c]), (2, piece[c], every)]
    wait = weight_copies(groups, (wo_own, we_own, wr_own), (wo_oth, we_oth, wr_oth),
                         (wo_ref, we_ref, wr_ref), sem, sel_ref[0])
    row = lambda i: vec_ref[i:i + 1, :]
    wait(0)
    hidden = x_ref[...].astype(F32) + (nn(att_ref[...], wo_ref[...]) + row(0))
    hat, rstd = norm_forward(hidden)
    hat1_ref[...] = hat
    rstd_ref[:, 0:1] = rstd
    first = hat * row(1) + row(2)
    low = first.astype(BF16)
    first_ref[...] = low
    down = first + row(7)
    for c in range(chunks):
        wait(1 + 2 * c)
        up = nn(low, we_ref[:, piece[c]]) + row(3 + c)
        cdf = 0.5 * (1.0 + erf(up * (2.0 ** -0.5)))
        act = (up * cdf).astype(BF16)
        slope_ref[:, piece[c]] = cdf + up * (jnp.exp(-0.5 * up * up) * 0.3989422804014327)
        act_ref[:, piece[c]] = act
        wait(2 + 2 * c)
        down = down + nn(act, wr_ref[piece[c], :])
    hat, rstd = norm_forward(down)
    hat2_ref[...] = hat
    rstd_ref[:, 1:2] = rstd
    valid = lax.broadcasted_iota(jnp.int32, (rows, width), 0) < sel_ref[1]
    y_ref[...] = jnp.where(valid, hat * row(8) + row(9), 0.0).astype(BF16)


def post_backward(
    sel_ref, g_ref, hat1_ref, hat2_ref, rstd_ref, slope_ref, vec_ref,
    wo_own, we_own, wr_own, wo_oth, we_oth, wr_oth,
    gd_ref, gu_ref, gp_ref, gr_ref, do_ref, sums_ref,
    wo_ref, we_ref, wr_ref, sem):
    rows, width = g_ref.shape
    chunks = gu_ref.shape[1] // width
    every = pl.ds(0, width)
    piece = [pl.ds(c * width, width) for c in range(chunks)]
    groups = []
    for c in range(chunks):
        groups += [(2, piece[c], every), (1, every, piece[c])]
    groups.append((0, every, every))
    wait = weight_copies(groups, (wo_own, we_own, wr_own), (wo_oth, we_oth, wr_oth),
                         (wo_ref, we_ref, wr_ref), sem, sel_ref[0])
    row = lambda i: vec_ref[i:i + 1, :]

    def total(i, values):
        sums_ref[i:i + 1, :] = jnp.sum(values, axis=0, keepdims=True)

    valid = lax.broadcasted_iota(jnp.int32, (rows, width), 0) < sel_ref[1]
    g = jnp.where(valid, g_ref[...].astype(F32), 0.0)
    hat2 = hat2_ref[...]
    total(8, g * hat2)
    total(9, g)
    second = norm_back(g * row(8), hat2, rstd_ref[:, 1:2])
    gd = second.astype(BF16)
    gd_ref[...] = gd
    total(7, gd.astype(F32))
    grad = second
    for c in range(chunks):
        wait(2 * c)
        gu = (nt(gd, wr_ref[piece[c], :]) * slope_ref[:, piece[c]]).astype(BF16)
        gu_ref[:, piece[c]] = gu
        total(3 + c, gu.astype(F32))
        wait(2 * c + 1)
        grad = grad + nt(gu, we_ref[:, piece[c]])
    hat1 = hat1_ref[...]
    total(1, grad * hat1)
    total(2, grad)
    residual = norm_back(grad * row(1), hat1, rstd_ref[:, 0:1])
    gr_ref[...] = residual
    gp = residual.astype(BF16)
    gp_ref[...] = gp
    total(0, gp.astype(F32))
    wait(2 * chunks)
    do_ref[...] = nt(gp, wo_ref[...])


def partner_of(bit):
    me = lax.axis_index("batch")
    side = (me // (1 << bit)) % 2
    return me + (1 - 2 * side) * (1 << bit), side


def place_of(block, order):
    last = len(order) - 1
    return sum(((block >> bit) & 1) << (last - k) for k, bit in enumerate(order))


def reduce_weights(*refs, owner, orders):
    count, bits = len(orders), len(orders[0])
    xs, ys = refs[:count], refs[count:2 * count]
    vec_ref = refs[2 * count]
    outs = refs[2 * count + 1:3 * count + 1]
    vec_out = refs[3 * count + 1]
    rest = refs[3 * count + 2:]
    xr, yr = rest[:count], rest[count:2 * count]
    grads = rest[2 * count:3 * count]
    got = rest[3 * count:4 * count]
    vec_got, vec_sum, op_send, op_recv, rs_send, rs_recv, v_send, v_recv = rest[4 * count:]
    mine = lax.axis_index("section") == owner
    barrier = pltpu.get_barrier_semaphore()

    def operand(i, first):
        source, target = (xs[i], xr[i]) if first else (ys[i], yr[i])
        slot = 2 * i + (0 if first else 1)
        return pltpu.make_async_remote_copy(
            src_ref=source, dst_ref=target, send_sem=op_send.at[slot], recv_sem=op_recv.at[slot],
            device_id={"section": owner}, device_id_type=MESH)

    def vec_in():
        return pltpu.make_async_remote_copy(
            src_ref=vec_ref, dst_ref=vec_got.at[bits], send_sem=v_send.at[bits],
            recv_sem=v_recv.at[bits], device_id={"section": owner}, device_id_type=MESH)

    @pl.when(jnp.logical_not(mine))
    def _():
        pl.semaphore_wait(barrier, 1)
        for i in range(count):
            operand(i, True).start()
            operand(i, False).start()
        vec_in().start()
        for i in range(count):
            operand(i, True).wait_send()
            operand(i, False).wait_send()
        vec_in().wait_send()

    @pl.when(mine)
    def _():
        pl.semaphore_signal(barrier, inc=1, device_id={"section": 1 - owner}, device_id_type=MESH)
        for bit in range(bits):
            pl.semaphore_signal(
                barrier, inc=1, device_id={"batch": partner_of(bit)[0]}, device_id_type=MESH)
        pl.semaphore_wait(barrier, bits)

        def spans(i, stage):
            order = orders[i]
            half = 1 << (bits - 1 - stage)
            start = 0
            for k in range(stage):
                start = start + partner_of(order[k])[1] * (1 << (bits - 1 - k))
            side = partner_of(order[stage])[1]
            landing = (1 << bits) - 2 * half
            return half, start + side * half, start + (1 - side) * half, landing

        def hop(i, stage):
            half, _, away, landing = spans(i, stage)
            return pltpu.make_async_remote_copy(
                src_ref=grads[i].at[pl.ds(away, half)], dst_ref=got[i].at[pl.ds(landing, half)],
                send_sem=rs_send.at[i, stage], recv_sem=rs_recv.at[i, stage],
                device_id={"batch": partner_of(orders[i][stage])[0]}, device_id_type=MESH)

        def vec_hop(stage):
            return pltpu.make_async_remote_copy(
                src_ref=vec_sum.at[stage], dst_ref=vec_got.at[stage],
                send_sem=v_send.at[stage], recv_sem=v_recv.at[stage],
                device_id={"batch": partner_of(stage)[0]}, device_id_type=MESH)

        vec_in().wait_recv()
        vec_sum[0] = vec_ref[...] + vec_got[bits]
        vec_hop(0).start()
        for i in range(count):
            operand(i, True).wait_recv()
            operand(i, False).wait_recv()
            depth, columns = xs[i].shape[1], ys[i].shape[1]
            block = grads[i].shape[1]
            rows = block * 128 // math.gcd(block, 128)
            step = min(columns, 768)
            for base in range(0, depth, rows):
                left = cat([xs[i][:, base:base + rows], xr[i][:, base:base + rows]], 0)
                for c in range(0, columns, step):
                    right = cat([ys[i][:, c:c + step], yr[i][:, c:c + step]], 0)
                    value = tn(left, right).astype(BF16)
                    for j in range(rows // block):
                        spot = place_of(base // block + j, orders[i])
                        grads[i][spot, :, c:c + step] = value[j * block:(j + 1) * block]
            hop(i, 0).start()
        for stage in range(bits):
            vec_hop(stage).wait_recv()
            vec_sum[stage + 1] = vec_sum[stage] + vec_got[stage]
            if stage + 1 < bits:
                vec_hop(stage + 1).start()
            for i in range(count):
                half, keep, _, landing = spans(i, stage)
                hop(i, stage).wait_recv()
                if stage + 1 < bits:
                    def add(j, carry):
                        grads[i][keep + j] = (
                            grads[i][keep + j].astype(F32) + got[i][landing + j].astype(F32)
                        ).astype(BF16)
                        return carry

                    lax.fori_loop(0, half, add, 0)
                    hop(i, stage + 1).start()
                else:
                    outs[i][...] = grads[i][keep].astype(F32) + got[i][landing].astype(F32)
        vec_out[...] = vec_sum[bits]
        for stage in range(bits):
            vec_hop(stage).wait_send()
            for i in range(count):
                hop(i, stage).wait_send()


def shape(dims, kind=F32):
    return jax.ShapeDtypeStruct(dims, kind)


IN_VMEM = pl.BlockSpec(memory_space=pltpu.VMEM)
IN_SMEM = pl.BlockSpec(memory_space=pltpu.SMEM)
ANYWHERE = pl.BlockSpec(memory_space=pl.ANY)
VMEM_LIMIT = 60 * 2 ** 20


def call(kernel, name, ins, outs, scratch, args, flops, moved, collective=None):
    extra = {} if collective is None else dict(collective_id=collective, has_side_effects=True)
    return pl.pallas_call(
        kernel, out_shape=tuple(outs), in_specs=ins, out_specs=(IN_VMEM,) * len(outs),
        scratch_shapes=scratch, name=name,
        cost_estimate=pl.CostEstimate(flops=flops, bytes_accessed=moved, transcendentals=0),
        compiler_params=pltpu.CompilerParams(vmem_limit_bytes=VMEM_LIMIT, **extra))(*args)


def forward_layer(sel, x, weights, others, vec, bias, taps_row, taps):
    rows, width = x.shape
    pairs, heads = width // PAIR, width // LM
    hidden = weights[2].shape[1]
    attended, qkv, lm, a1, a2, a3, band, newton, db, err = call(
        functools.partial(attention_forward, taps=taps), "attention_forward",
        [IN_SMEM] + [IN_VMEM] * 3 + [ANYWHERE] * 2,
        [shape((rows, width), BF16), shape((3, rows, width), BF16), shape((2, LM, width), BF16),
         shape((rows, width)), shape((LM, width)), shape((LM, heads * rows)),
         shape((pairs, rows, 2 * rows)), shape((4, NEWTON + 1, LM, width)),
         shape((2, LM, width), BF16), shape((NEWTON, 1, width))],
        [pltpu.VMEM((width, 3 * width), BF16), pltpu.SemaphoreType.DMA((3,))],
        (sel, x, bias, taps_row, weights[0], others[0]), 10 ** 10, 10 ** 7)
    chunks = hidden // width
    y, first, act, hat1, hat2, rstd, slope = call(
        post_forward, "post_forward",
        [IN_SMEM] + [IN_VMEM] * 3 + [ANYWHERE] * 6,
        [shape((rows, width), BF16), shape((rows, width), BF16), shape((rows, hidden), BF16),
         shape((rows, width)), shape((rows, width)), shape((rows, 128)), shape((rows, hidden))],
        [pltpu.VMEM((width, width), BF16), pltpu.VMEM((width, hidden), BF16),
         pltpu.VMEM((hidden, width), BF16), pltpu.SemaphoreType.DMA((1 + 2 * chunks,))],
        (sel, attended, x, vec) + tuple(weights[1:]) + tuple(others[1:]), 2 * 10 ** 9, 10 ** 7)
    kept = dict(x=x, attended=attended, attention=(qkv, lm, a1, a2, a3, band, newton, db),
                first=first, act=act, post=(hat1, hat2, rstd, slope))
    return y, err, kept


def backward_layer(sel, grad, kept, weights, others, vec, taps):
    rows, width = grad.shape
    hidden = weights[2].shape[1]
    chunks = hidden // width
    hat1, hat2, rstd, slope = kept["post"]
    gd, gu, gp, residual, d_attended, sums = call(
        post_backward, "post_backward",
        [IN_SMEM] + [IN_VMEM] * 6 + [ANYWHERE] * 6,
        [shape((rows, width), BF16), shape((rows, hidden), BF16), shape((rows, width), BF16),
         shape((rows, width)), shape((rows, width)), shape((4 + 2 + chunks, width))],
        [pltpu.VMEM((width, width), BF16), pltpu.VMEM((width, hidden), BF16),
         pltpu.VMEM((hidden, width), BF16), pltpu.SemaphoreType.DMA((1 + 2 * chunks,))],
        (sel, grad, hat1, hat2, rstd, slope, vec) + tuple(weights[1:]) + tuple(others[1:]),
        2 * 10 ** 9, 10 ** 7)
    heads = width // LM
    dqkv, gi, cols, dtaps = call(
        functools.partial(attention_backward, taps=taps), "attention_backward",
        [IN_SMEM] + [IN_VMEM] * 10 + [ANYWHERE] * 2,
        [shape((rows, 3 * width), BF16), shape((rows, width), BF16), shape((3, width)),
         shape((16, rows))],
        [pltpu.VMEM((3, width, width), BF16), pltpu.VMEM((LM, width), F32),
         pltpu.VMEM((LM, width), F32), pltpu.VMEM((LM, width), F32), pltpu.SemaphoreType.DMA((3,))],
        (sel, d_attended, residual) + kept["attention"] + (weights[0], others[0]),
        10 ** 10, 10 ** 7)
    xs = (kept["act"], kept["first"], kept["x"], kept["attended"])
    ys = (gd, gu, dqkv, gp)
    return gi, xs, ys, sums, cols, dtaps[:heads]


def small_rows(sums, cols, dtaps, err, width):
    residuals = jnp.pad(jnp.sum(err, axis=(1, 2)), (0, width - NEWTON))
    return jnp.concatenate([
        sums, cols[0:1], cols[2:3], dtaps.reshape(-1, width), residuals[None],
        jnp.zeros((16 - sums.shape[0] - 3 - dtaps.size // width, width), F32)], axis=0)


def reduce_on_slice(owner, xs, ys, small, batch):
    bits = batch.bit_length() - 1
    count = len(xs)
    first = (0, 1, 2)
    orders = []
    for i in (0, 1, 2, 2):
        turned = [first[i], first[(i + 1) % 3], first[(i + 2) % 3]]
        orders.append(tuple(turned + list(range(3, bits))))
    blocks = [x.shape[1] // batch for x in xs]
    outs = [shape((b, y.shape[1])) for b, y in zip(blocks, ys)] + [shape(small.shape)]
    scratch = [pltpu.VMEM(x.shape, BF16) for x in xs] + [pltpu.VMEM(y.shape, BF16) for y in ys]
    scratch += [pltpu.VMEM((batch, b, y.shape[1]), BF16) for b, y in zip(blocks, ys)]
    scratch += [pltpu.VMEM((batch - 1, b, y.shape[1]), BF16) for b, y in zip(blocks, ys)]
    scratch += [pltpu.VMEM((bits + 1,) + small.shape, F32), pltpu.VMEM((bits + 1,) + small.shape, F32)]
    dma = pltpu.SemaphoreType.DMA
    scratch += [dma((2 * count,)), dma((2 * count,)), dma((count, bits)), dma((count, bits)),
                dma((bits + 1,)), dma((bits + 1,))]
    return call(
        functools.partial(reduce_weights, owner=owner, orders=tuple(orders)),
        "reduce_weights", [IN_VMEM] * (2 * count + 1), outs, scratch,
        tuple(xs) + tuple(ys) + (small,), 4 * 10 ** 9, 10 ** 7, collective=owner)


def swap(value):
    return lax.ppermute(value, "section", [(0, 1), (1, 0)])


def body(
    layer_input, seq_lengths, cotangent, project_weight, project_bias, conv_kernel, output_weight,
    output_bias, attn_gain, attn_shift, expand_weight, expand_bias, reduce_weight, reduce_bias,
    final_gain, final_shift):
    section = lax.axis_index("section")
    batch = lax.axis_size("batch")
    lead = section == 0
    total, width = layer_input.shape
    rows = total // seq_lengths.shape[0]
    heads, taps = conv_kernel.shape[1:]
    weights = (project_weight[0], output_weight[0], expand_weight[0], reduce_weight[0])
    others = tuple(swap(w) for w in weights)
    tap_rows = jnp.pad(conv_kernel[0], ((0, 0), (0, 128 - taps)))
    pieces = [output_bias, attn_gain, attn_shift, expand_bias.reshape(-1, width), reduce_bias,
              final_gain, final_shift, project_bias.reshape(2, width),
              tap_rows.reshape(-1, width)]
    vec = jnp.concatenate(pieces, axis=0)
    vec_other = swap(vec)
    count = seq_lengths.shape[0]
    length = lax.dynamic_index_in_dim(seq_lengths, section, keepdims=False)
    own_rows = lambda v: lax.dynamic_slice_in_dim(v, section * rows, rows, 0)
    sels, vecs, biases, tap_list = [], [], [], []
    for layer in range(2):
        here = section == layer
        sels.append(jnp.stack([here.astype(jnp.int32), length]))
        v = jnp.where(here, vec, vec_other)
        vecs.append(v)
        biases.append(jnp.stack([v[10], jnp.zeros_like(v[10]), v[11]]))
        t = v[12:].reshape(heads, 128)
        tap_list.append(jnp.pad(t, ((0, 16 - heads), (0, 0))))
    value = own_rows(layer_input)
    outputs, residuals, kept = [], [], []
    for layer in range(2):
        value, err, saved = forward_layer(
            sels[layer], value, weights, others, vecs[layer], biases[layer], tap_list[layer], taps)
        outputs.append(value)
        residuals.append(err)
        kept.append(saved)
    crossed = swap(jnp.where(lead, outputs[1], outputs[0]))
    activations = jnp.where(
        lead, jnp.concatenate([outputs[0], crossed]), jnp.concatenate([crossed, outputs[1]]))
    grad = own_rows(cotangent)
    shares, grads = [None, None], [None, None]
    for layer in (1, 0):
        grad, xs, ys, sums, cols, dtaps = backward_layer(
            sels[layer], grad, kept[layer], weights, others, vecs[layer], taps)
        grads[layer] = grad
        small = small_rows(sums, cols, dtaps, residuals[layer], width)
        shares[layer] = reduce_layer(layer, xs, ys, small, batch)
    crossed = swap(jnp.where(lead, grads[1], grads[0]))
    input_grads = jnp.where(
        lead, jnp.concatenate([grads[0], crossed]), jnp.concatenate([crossed, grads[1]]))
    g_red, g_exp, g_qkv, g_out, small = [
        jnp.where(lead, a, b) for a, b in zip(shares[0], shares[1])]
    index = lax.axis_index("batch")

    def share(first, many):
        flat = small[first:first + many].reshape(-1)
        size = flat.shape[0] // batch
        return lax.dynamic_slice_in_dim(flat, index * size, size, 0)[None]

    chunks = reduce_weight.shape[1] // width
    at = 6 + chunks
    dtaps = small[at + 2:at + 2 + heads * 128 // width].reshape(heads, 128)[:, :taps]
    proxies = small[at + 2 + heads * 128 // width, :NEWTON]
    return (
        activations[None], input_grads[None], g_qkv[None], share(at, 2), dtaps[None], g_out[None],
        share(0, 1), share(1, 1), share(2, 1), g_exp[None], share(3, chunks), g_red[None],
        share(3 + chunks, 1), share(4 + chunks, 1), share(5 + chunks, 1), proxies[None])


def reduce_layer(layer, xs, ys, small, batch):
    if all((x.shape[1] // batch) % 16 == 0 for x in xs) and batch >= 8:
        return reduce_on_slice(layer, xs, ys, small, batch)
    products = [lax.dot_general(x, y, (((0,), (0,)), ((), ())), preferred_element_type=F32)
                for x, y in zip(xs, ys)]
    return [lax.psum_scatter(lax.psum(p, "section"), "batch", scatter_dimension=0, tiled=True)
            for p in products] + [lax.psum(small, ("section", "batch"))]


def solution(mesh):
    split_rows = P("batch", None)
    two, three = P("section", None), P("section", None, None)
    return jax.shard_map(
        body, mesh=mesh,
        in_specs=(split_rows, P("batch"), split_rows, three, two, three, three, two, two, two,
                  three, two, three, two, two, two),
        out_specs=(P("section", "batch", None), P("section", "batch", None),
                   P("section", "batch", None), P("section", "batch"), three,
                   P("section", "batch", None), P("section", "batch"), P("section", "batch"),
                   P("section", "batch"), P("section", "batch", None), P("section", "batch"),
                   P("section", "batch", None), P("section", "batch"), P("section", "batch"),
                   P("section", "batch"), two),
        check_vma=False)
```

time: 1130 us -> 345 us (0.31)
  waiting for transfers between devices: 441 us -> 8.8 us
  matrix products: 356 us -> 0 us
  Pallas kernels: 0 us -> 287 us
  other arithmetic: 122 us -> 13.7 us
  blocking collectives: 81 us -> 0 us
  local copies, waits for them, and re-layouts: 80.9 us -> 27.9 us
  between operations: 33.9 us -> 1.22 us
    reduce_scatter x4 -> x0, waiting for transfers between devices: 439 us -> none  [body(): shares = lax.psum_scatter(totals, 'batch', scatter_dimension=0, tiled=True)]
    dot_general x321 -> x0, matrix products: 356 us -> none  [the longest x108 76.6 us: newton_inverse(): jnp.matmul(product, factor, precision=MAXIMAL_PRECISION)]
    pallas_call x0 -> x10, Pallas kernels: none -> 287 us  [call(): pl.pallas_call(kernel, out_shape=tuple(outs), in_specs=ins, out_specs=(IN...]
    unnamed x1 -> x0, blocking collectives: 81 us -> none
    mul x20 -> x0, other arithmetic: 28.7 us -> none  [the longest x6 13.8 us: attention(): kernel_taps[:, tap_index][None, :, None]]
    add_any x3 -> x0, other arithmetic: 25.5 us -> none  [attention(): padded[tap_index:tap_index + slot_rows]]
    reduce_sum x33 -> x2, other arithmetic: 26.5 us -> 1.72 us  [small_rows(): residuals = jnp.pad(jnp.sum(err, axis=(1, 2)), (0, width - NEWTON))]
    mul x9 -> x0, local copies, waits for them, and re-layouts: 17.3 us -> none  [the longest x3 5.81 us: attention(): qkv_rows[:, 2 * model_width:] * valid_rows]
  transfers between devices with their start and end apart: 8 -> 7, of which waited for: 6 -> 1; matrix products, arithmetic and copies ran while one was open for 11% -> 6% of each run, Pallas kernels for 0% -> 6%
where the time goes in v1:
time: 345 us; the launch traced here: 340 us
  Pallas kernels  287 us (83%)
  local copies, waits for them, and re-layouts  27.9 us (8%)
  other arithmetic  13.7 us (4%)
  waiting for transfers between devices  8.8 us (3%)
    pallas_call x10, Pallas kernels, call(): pl.pallas_call(kernel, out_shape=tuple(outs), in_specs=ins, out_specs=(IN...  287 us
    ppermute x7, waiting for transfers between devices, swap(): return lax.ppermute(value, 'section', [(0, 1), (1, 0)])  8.8 us
    dynamic_slice x7, local copies, waits for them, and re-layouts, share(): return lax.dynamic_slice_in_dim(flat, index * size, size, 0)[None]  8.2 us
  transfers between devices with their start and end apart: 7, of which 1 were waited for; matrix products, arithmetic and copies ran while one was open for 6% of the time, Pallas kernels for 6%

profile of v1, /device:TPU:0, one launch (start us, length us, event | category | flops | bytes accessed | tf_op | source)
XLA Modules:
  0.0 340.5 jit_solution(2410034274305848540)
XLA Ops:
  3.6 1.4 reduce.4
  5.0 1.5 concatenate.61
  9.0 1.6 constant_dynamic-slice_fusion.6.g_ref
  13.8 8.8 %collective-permute-done.1.other_ref = bf16[768,2304]{1,0:T(8,128)(2,1)} collective-permute-done((bf16[768,2304]{1,0:T(8,128)(2,1)}, bf16[768,2304]{1,0:T(8,128)(2,1)}, u32[]{:S(2)}, u32[]{:S(2)}) %collective-permute-start.1) | collective-permute-done | bytes 3538976 | tf_op jit(solution)/shard_map/ppermute | solution.py:716
  22.6 21.8 %attention_forward.2 = (bf16[128,768]{1,0:T(8,128)(2,1)}, bf16[3,128,768]{2,1,0:T(8,128)(2,1)}, bf16[2,64,768]{2,1,0:T(8,128)(2,1)}, f32[128,768]{1,0:T(8,128)},...) custom-call(s32[2]{0:T(128)} %get-tuple-element.164.sel_ref, ...), custom_call_target="tpu_custom_call" | custom-call | flops 10000000000 | bytes 10000000 | tf_op jit(solution)/shard_map/attention_forward/pallas_call | solution.py:622
  46.3 7.3 %post_forward.2 = (bf16[128,768]{1,0:T(8,128)(2,1)}, bf16[128,768]{1,0:T(8,128)(2,1)}, bf16[128,3072]{1,0:T(8,128)(2,1)}, f32[128,768]{1,0:T(8,128)}, f32[128,76...) custom-call(s32[2]{0:T(128)} %get-tuple-element.164.sel_ref, ...), custom_call_target="tpu_custom_call" | custom-call | flops 2000000000 | bytes 10000000 | tf_op jit(solution)/shard_map/post_forward/pallas_call | solution.py:622
  53.6 21.9 %attention_forward.3 = (bf16[128,768]{1,0:T(8,128)(2,1)}, bf16[3,128,768]{2,1,0:T(8,128)(2,1)}, bf16[2,64,768]{2,1,0:T(8,128)(2,1)}, f32[128,768]{1,0:T(8,128)},...) custom-call(s32[2]{0:T(128)} %get-tuple-element.165.sel_ref, ...), custom_call_target="tpu_custom_call" | custom-call | flops 10000000000 | bytes 10000000 | tf_op jit(solution)/shard_map/attention_forward/pallas_call | solution.py:622
  76.4 7.4 %post_forward.3 = (bf16[128,768]{1,0:T(8,128)(2,1)}, bf16[128,768]{1,0:T(8,128)(2,1)}, bf16[128,3072]{1,0:T(8,128)(2,1)}, f32[128,768]{1,0:T(8,128)}, f32[128,76...) custom-call(s32[2]{0:T(128)} %get-tuple-element.165.sel_ref, ...), custom_call_target="tpu_custom_call" | custom-call | flops 2000000000 | bytes 10000000 | tf_op jit(solution)/shard_map/post_forward/pallas_call | solution.py:622
  83.8 9.1 %post_backward.2 = (bf16[128,768]{1,0:T(8,128)(2,1)}, bf16[128,3072]{1,0:T(8,128)(2,1)}, bf16[128,768]{1,0:T(8,128)(2,1)}, f32[128,768]{1,0:T(8,128)}, f32[128,768]{1,0:T(8,128)}, /*index=5*/f32[10,768]{1,0:T(8,128)}) custom-call(s32[2]{0:T(128)} %get-tuple-element.165.sel_ref, bf16[128,768]{1,0:T(8,128)(2,1)} %constant_dynamic-slice_fusion.6.g_ref, ...), custom_call_target="tpu_custom_call" | custom-call | flops 2000000000 | bytes 10000000 | tf_op jit(solution)/shard_map/post_backward/pallas_call | solution.py:622
  93.0 20.3 %attention_backward.2 = (bf16[128,2304]{1,0:T(8,128)(2,1)}, bf16[128,768]{1,0:T(8,128)(2,1)}, f32[3,768]{1,0:T(4,128)}, f32[16,128]{1,0:T(8,128)}) custom-call(s32[2]{0:T(128)} %get-tuple-element.165.sel_ref, f32[128,768]{1,0:T(8,128)} %get-tuple-element.88.do_ref, f32[128,768]{1,0:T(8,128)} %get-tuple-element.89.gr_ref, ...), custom_call_target="tpu_custom_call" | custom-call | flops 10000000000 | bytes 10000000 | tf_op jit(solution)/shard_map/attention_backward/pallas_call | solution.py:622
  114.0 9.1 %post_backward.3 = (bf16[128,768]{1,0:T(8,128)(2,1)}, bf16[128,3072]{1,0:T(8,128)(2,1)}, bf16[128,768]{1,0:T(8,128)(2,1)}, f32[128,768]{1,0:T(8,128)}, f32[128,768]{1,0:T(8,128)}, /*index=5*/f32[10,768]{1,0:T(8,128)}) custom-call(s32[2]{0:T(128)} %get-tuple-element.164.sel_ref, bf16[128,768]{1,0:T(8,128)(2,1)} %get-tuple-element.98.g_ref, ...), custom_call_target="tpu_custom_call" | custom-call | flops 2000000000 | bytes 10000000 | tf_op jit(solution)/shard_map/post_backward/pallas_call | solution.py:622
  123.1 19.9 %attention_backward.3 = (bf16[128,2304]{1,0:T(8,128)(2,1)}, bf16[128,768]{1,0:T(8,128)(2,1)}, f32[3,768]{1,0:T(4,128)}, f32[16,128]{1,0:T(8,128)}) custom-call(s32[2]{0:T(128)} %get-tuple-element.164.sel_ref, f32[128,768]{1,0:T(8,128)} %get-tuple-element.103.do_ref, f32[128,768]{1,0:T(8,128)} %get-tuple-element.104.gr_ref, ...), custom_call_target="tpu_custom_call" | custom-call | flops 10000000000 | bytes 10000000 | tf_op jit(solution)/shard_map/attention_backward/pallas_call | solution.py:622
  144.6 2.0 concatenate.73.refs_8_
  146.6 2.0 concatenate.72.refs_8_
  148.6 9.8 %reduce_weights.3 = (f32[192,768]{1,0:T(8,128)}, f32[48,3072]{1,0:T(8,128)}, f32[48,2304]{1,0:T(8,128)}, f32[48,768]{1,0:T(8,128)}, f32[16,768]{1,0:T(8,128)}) custom-call(bf16[128,3072]{1,0:T(8,128)(2,1)} %get-tuple-element.125.refs_0_, bf16[128,768]{1,0:T(8,128)(2,1)} %get-tuple-element.126.refs_1_, bf16[128,768]{1,0:T(8,128)(2,1)} %get-tuple-element.81.x_ref.refs_2_, ...), custom_call_target="tpu_custom_call" | custom-call | flops 4000000000 | bytes 10000000 | tf_op jit(solution)/shard_map/reduce_weights/pallas_call | solution.py:622
  158.4 160.0 %reduce_weights.2 = (f32[192,768]{1,0:T(8,128)}, f32[48,3072]{1,0:T(8,128)}, f32[48,2304]{1,0:T(8,128)}, f32[48,768]{1,0:T(8,128)}, f32[16,768]{1,0:T(8,128)}) custom-call(bf16[128,3072]{1,0:T(8,128)(2,1)} %get-tuple-element.114.refs_0_, bf16[128,768]{1,0:T(8,128)(2,1)} %get-tuple-element.115.refs_1_, ...), custom_call_target="tpu_custom_call" | custom-call | flops 4000000000 | bytes 10000000 | tf_op jit(solution)/shard_map/reduce_weights/pallas_call | solution.py:622
  321.7 1.3 constant_dynamic-slice_fusion
  323.0 1.3 constant_dynamic-slice_fusion.1
  324.2 1.3 constant_dynamic-slice_fusion.2
  325.5 1.2 constant_dynamic-slice_fusion.3
  326.7 1.3 constant_dynamic-slice_fusion.4
  330.7 2.0 select_bitcast_fusion
  332.6 2.0 select_bitcast_fusion.1
  336.1 1.3 dynamic_slice.41
  (96 shorter events, 23.8 us)
Async XLA Ops:
  0.6 7.7 %copy-start = (bf16[256,768]{1,0:T(8,128)(2,1)S(1)}, bf16[256,768]{1,0:T(8,128)(2,1)}, u32[]{:S(2)}) copy-start(bf16[256,768]{1,0:T(8,128)(2,1)} %param.16) | copy-start | bytes 1179652
  0.7 44.7 %collective-permute-start.3 = (bf16[768,3072]{1,0:T(8,128)(2,1)}, bf16[768,3072]{1,0:T(8,128)(2,1)}, u32[]{:S(2)}, u32[]{:S(2)}) collective-permute-start(bf16[768,3072]{1,0:T(8,128)(2,1)} %bitcast.29), channel_id=1, source_target_pairs={{0,16},{16,0},{1,17},{17,1},{2,18},{18,2},{3,19},{19,3},{4,20},{20... | collective-permute-start | bytes 14155784 | tf_op jit(solution)/shard_map/ppermute | solution.py:716
  1.2 44.2 %collective-permute-start.4 = (bf16[3072,768]{1,0:T(8,128)(2,1)}, bf16[3072,768]{1,0:T(8,128)(2,1)}, u32[]{:S(2)}, u32[]{:S(2)}) collective-permute-start(bf16[3072,768]{1,0:T(8,128)(2,1)} %bitcast.34), channel_id=1, source_target_pairs={{0,16},{16,0},{1,17},{17,1},{2,18},{18,2},{3,19},{19,3},{4,20},{20... | collective-permute-start | bytes 14155784 | tf_op jit(solution)/shard_map/ppermute | solution.py:716
  1.3 21.4 %collective-permute-start.1 = (bf16[768,2304]{1,0:T(8,128)(2,1)}, bf16[768,2304]{1,0:T(8,128)(2,1)}, u32[]{:S(2)}, u32[]{:S(2)}) collective-permute-start(bf16[768,2304]{1,0:T(8,128)(2,1)} %bitcast.55), channel_id=1, source_target_pairs={{0,16},{16,0},{1,17},{17,1},{2,18},{18,2},{3,19},{19,3},{4,20},{20... | collective-permute-start | bytes 10616840 | tf_op jit(solution)/shard_map/ppermute | solution.py:716
  6.5 5.4 %collective-permute-start = (f32[14,768]{1,0:T(8,128)S(1)}, f32[14,768]{1,0:T(8,128)S(1)}, u32[]{:S(2)}, u32[]{:S(2)}) collective-permute-start(f32[14,768]{1,0:T(8,128)S(1)} %concatenate.61), channel_id=1, source_target_pairs={{0,16},{16,0},{1,17},{17,1},{2,18},{18,2},{3,19},{19,3},{4,20},{20... | collective-permute-start | bytes 129032 | tf_op jit(solution)/shard_map/ppermute | solution.py:716
  6.7 38.6 %collective-permute-start.2 = (bf16[768,768]{1,0:T(8,128)(2,1)}, bf16[768,768]{1,0:T(8,128)(2,1)S(1)}, u32[]{:S(2)}, u32[]{:S(2)}) collective-permute-start(bf16[768,768]{1,0:T(8,128)(2,1)} %bitcast.39), channel_id=1, source_target_pairs={{0,16},{16,0},{1,17},{17,1},{2,18},{18,2},{3,19},{19,3},{4,20},{20... | collective-permute-start | bytes 3538952 | tf_op jit(solution)/shard_map/ppermute | solution.py:716
  11.9 32.5 %copy-start.8 = (f32[14,768]{1,0:T(8,128)}, f32[14,768]{1,0:T(8,128)S(1)}, u32[]{:S(2)}) copy-start(f32[14,768]{1,0:T(8,128)S(1)} %get-tuple-element.145.vec_ref) | copy-start | bytes 129028
  11.9 32.5 %copy-start.9 = (f32[14,768]{1,0:T(8,128)}, f32[14,768]{1,0:T(8,128)S(1)}, u32[]{:S(2)}) copy-start(f32[14,768]{1,0:T(8,128)S(1)} %get-tuple-element.144.vec_ref) | copy-start | bytes 129028
  123.1 20.7 %copy-start.17 = (f32[3,768]{1,0:T(4,128)S(1)}, f32[3,768]{1,0:T(4,128)}, u32[]{:S(2)}) copy-start(f32[3,768]{1,0:T(4,128)} %get-tuple-element.132) | copy-start | bytes 27652
  123.1 21.5 %copy-start.14 = (f32[10,768]{1,0:T(8,128)S(1)}, f32[10,768]{1,0:T(8,128)}, u32[]{:S(2)}) copy-start(f32[10,768]{1,0:T(8,128)} %get-tuple-element.131) | copy-start | bytes 92164
  123.1 23.5 %copy-start.15 = (f32[10,768]{1,0:T(8,128)S(1)}, f32[10,768]{1,0:T(8,128)}, u32[]{:S(2)}) copy-start(f32[10,768]{1,0:T(8,128)} %get-tuple-element.120) | copy-start | bytes 92164
  158.4 160.1 %copy-start.16 = (f32[16,768]{1,0:T(8,128)S(1)}, f32[16,768]{1,0:T(8,128)}, u32[]{:S(2)}) copy-start(f32[16,768]{1,0:T(8,128)} %get-tuple-element.137) | copy-start | bytes 147460
  158.4 171.6 %copy-start.3 = (bf16[128,768]{1,0:T(8,128)(2,1)S(1)}, bf16[128,768]{1,0:T(8,128)(2,1)}, u32[]{:S(2)}) copy-start(bf16[128,768]{1,0:T(8,128)(2,1)} %get-tuple-element.98.g_ref) | copy-start | bytes 589828
  158.4 171.6 %copy-start.5 = (bf16[128,768]{1,0:T(8,128)(2,1)S(1)}, bf16[128,768]{1,0:T(8,128)(2,1)}, u32[]{:S(2)}) copy-start(bf16[128,768]{1,0:T(8,128)(2,1)} %get-tuple-element.113) | copy-start | bytes 589828
  158.4 171.6 %copy-start.2 = (bf16[128,768]{1,0:T(8,128)(2,1)S(1)}, bf16[128,768]{1,0:T(8,128)(2,1)}, u32[]{:S(2)}) copy-start(bf16[128,768]{1,0:T(8,128)(2,1)} %get-tuple-element.81.x_ref.refs_2_) | copy-start | bytes 589828
  158.4 171.6 %copy-start.4 = (bf16[128,768]{1,0:T(8,128)(2,1)S(1)}, bf16[128,768]{1,0:T(8,128)(2,1)}, u32[]{:S(2)}) copy-start(bf16[128,768]{1,0:T(8,128)(2,1)} %get-tuple-element.83) | copy-start | bytes 589828
  158.4 172.3 %copy-start.7 = (f32[192,768]{1,0:T(8,128)S(1)}, f32[192,768]{1,0:T(8,128)}, u32[]{:S(2)}) copy-start(f32[192,768]{1,0:T(8,128)} %get-tuple-element.143) | copy-start | bytes 1769476
  158.4 174.2 %copy-start.6 = (f32[48,3072]{1,0:T(8,128)S(1)}, f32[48,3072]{1,0:T(8,128)}, u32[]{:S(2)}) copy-start(f32[48,3072]{1,0:T(8,128)} %get-tuple-element.141) | copy-start | bytes 1769476
  318.4 16.2 %copy-start.12 = (f32[48,768]{1,0:T(8,128)S(1)}, f32[48,768]{1,0:T(8,128)}, u32[]{:S(2)}) copy-start(f32[48,768]{1,0:T(8,128)} %get-tuple-element.139) | copy-start | bytes 442372
  318.4 16.2 %copy-start.13 = (f32[48,768]{1,0:T(8,128)S(1)}, f32[48,768]{1,0:T(8,128)}, u32[]{:S(2)}) copy-start(f32[48,768]{1,0:T(8,128)} %get-tuple-element.138) | copy-start | bytes 442372
  318.4 16.8 %copy-start.10 = (f32[48,2304]{1,0:T(8,128)S(1)}, f32[48,2304]{1,0:T(8,128)}, u32[]{:S(2)}) copy-start(f32[48,2304]{1,0:T(8,128)} %get-tuple-element.135) | copy-start | bytes 1327108
  318.4 16.8 %copy-start.11 = (f32[48,2304]{1,0:T(8,128)S(1)}, f32[48,2304]{1,0:T(8,128)}, u32[]{:S(2)}) copy-start(f32[48,2304]{1,0:T(8,128)} %get-tuple-element.124) | copy-start | bytes 1327108
  330.1 8.5 %collective-permute-start.5 = (bf16[128,768]{1,0:T(8,128)(2,1)S(1)}, bf16[128,768]{1,0:T(8,128)(2,1)S(1)}, u32[]{:S(2)}, u32[]{:S(2)}) collective-permute-start(bf16[128,768]{1,0:T(8,128)(2,1)S(1)} %broadcast_select_fusion.1), channel_id=1, source_target_pairs={{0,16},{16,0},{1,17},{17,1},{2,18},{18,2},{3,19},{19,3},{4,20},{20... | collective-permute-start | bytes 589832 | tf_op jit(solution)/shard_map/ppermute | solution.py:716
  330.2 9.3 %collective-permute-start.6 = (bf16[128,768]{1,0:T(8,128)(2,1)S(1)}, bf16[128,768]{1,0:T(8,128)(2,1)S(1)}, u32[]{:S(2)}, u32[]{:S(2)}) collective-permute-start(bf16[128,768]{1,0:T(8,128)(2,1)S(1)} %broadcast_select_fusion), channel_id=1, source_target_pairs={{0,16},{16,0},{1,17},{17,1},{2,18},{18,2},{3,19},{19,3},{4,20},{20... | collective-permute-start | bytes 589832 | tf_op jit(solution)/shard_map/ppermute | solution.py:716
  (1 other events, 1.0 us)

commit v2 on v1

--- a/solution.py
+++ b/solution.py
@@ -493,43 +493,207 @@
     return sum(((block >> bit) & 1) << (last - k) for k, bit in enumerate(order))
 
 
-def reduce_weights(*refs, owner, orders):
-    count, bits = len(orders), len(orders[0])
-    xs, ys = refs[:count], refs[count:2 * count]
-    vec_ref = refs[2 * count]
-    outs = refs[2 * count + 1:3 * count + 1]
-    vec_out = refs[3 * count + 1]
-    rest = refs[3 * count + 2:]
-    xr, yr = rest[:count], rest[count:2 * count]
-    grads = rest[2 * count:3 * count]
-    got = rest[3 * count:4 * count]
-    vec_got, vec_sum, op_send, op_recv, rs_send, rs_recv, v_send, v_recv = rest[4 * count:]
+class Weight:
+    def __init__(self, owner, order, by_rows):
+        self.owner, self.order, self.by_rows = owner, order, by_rows
+        self.bits = len(order)
+        self.batch = 1 << self.bits
+        self.rest = order[1:] if by_rows else order[1:] + order[:1]
+        self.stages = self.bits - 1 if by_rows else self.bits
+
+    def sizes(self, x, y):
+        self.block = x[1] // self.batch
+        self.run = (1 << self.order[0]) * self.block
+        self.runs = self.batch >> (self.order[0] + 1) if self.by_rows else 1
+        self.rows, self.depth, self.width = x[0], x[1], y[1]
+        self.deep = self.depth // 2 if self.by_rows else self.depth
+        self.wide = self.width if self.by_rows else self.width // 2
+        self.blocks = self.batch // 2 if self.by_rows else self.batch
+        return self
+
+    def scratch(self):
+        dma = pltpu.SemaphoreType.DMA
+        return [
+            pltpu.VMEM((3, self.rows, self.deep), BF16), pltpu.VMEM((3, self.rows, self.wide), BF16),
+            pltpu.VMEM((self.blocks, self.block, self.wide), BF16),
+            pltpu.VMEM((self.blocks - 1 if self.by_rows else self.blocks - 1, self.block, self.wide), BF16),
+            dma((2, self.runs + 1)), dma((3, self.runs + 1)), dma((self.stages,)), dma((self.stages,))]
+
+    def bind(self, x, y, out, scratch):
+        self.x, self.y, self.out = x, y, out
+        (self.xr, self.yr, self.sums, self.got,
+         self.op_send, self.op_recv, self.hop_send, self.hop_recv) = scratch
+        return self
+
+    def side(self):
+        return partner_of(self.order[0])[1]
+
+    def pieces(self, ref, side, first):
+        if first and self.by_rows:
+            for r in range(self.runs):
+                start = pl.multiple_of(2 * r * self.run + side * self.run, 128)
+                yield ref.at[:, pl.ds(start, self.run)], pl.ds(r * self.run, self.run)
+        elif first or self.by_rows:
+            yield ref, pl.ds(0, ref.shape[1])
+        else:
+            yield ref.at[:, pl.ds(pl.multiple_of(side * self.wide, 128), self.wide)], pl.ds(0, self.wide)
+
+    def operand(self, slot, away):
+        other, side = partner_of(self.order[0])
+        target = {"section": self.owner, "batch": other} if away else {"section": self.owner}
+        side = 1 - side if away else side
+        k = 0
+        for first, ref, into in ((True, self.x, self.xr), (False, self.y, self.yr)):
+            for source, lanes in self.pieces(ref, side, first):
+                yield pltpu.make_async_remote_copy(
+                    src_ref=source, dst_ref=into.at[slot, :, lanes],
+                    send_sem=self.op_send.at[1 if away else 0, k], recv_sem=self.op_recv.at[slot, k],
+                    device_id=target, device_id_type=MESH)
+                k += 1
+
+    def send_from_owner(self):
+        for copy in self.operand(1, True):
+            copy.start()
+
+    def send_from_other(self):
+        for slot, away in ((0, False), (2, True)):
+            for copy in self.operand(slot, away):
+                copy.start()
+
+    def sent_from_other(self):
+        for slot, away in ((0, False), (2, True)):
+            for copy in self.operand(slot, away):
+                copy.wait_send()
+
+    def multiply(self):
+        for slot, away in ((0, False), (1, True), (2, True)):
+            for copy in self.operand(slot, away):
+                copy.wait_recv()
+        side = self.side()
+        rows = self.block * 128 // math.gcd(self.block, 128)
+        step = max(s for s in range(128, 1153, 128) if self.wide % s == 0)
+        for base in range(0, self.deep, rows):
+            if self.by_rows:
+                r, inside = base // self.run, base % self.run
+                lanes = pl.ds(pl.multiple_of(2 * r * self.run + side * self.run + inside, 128), rows)
+            else:
+                lanes = pl.ds(base, rows)
+            left = cat([self.x[:, lanes]] + [self.xr[s, :, base:base + rows] for s in range(3)], 0)
+            for c in range(0, self.wide, step):
+                if self.by_rows:
+                    near = self.y[:, c:c + step]
+                else:
+                    near = self.y[:, pl.ds(pl.multiple_of(side * self.wide + c, 128), step)]
+                right = cat([near] + [self.yr[s, :, c:c + step] for s in range(3)], 0)
+                value = tn(left, right).astype(BF16)
+                for j in range(rows // self.block):
+                    block = base // self.block + j
+                    if self.by_rows:
+                        low = 1 << self.order[0]
+                        block = block // low * 2 * low + block % low
+                    self.sums[place_of(block, self.rest), :, c:c + step] = (
+                        value[j * self.block:(j + 1) * self.block])
+        self.hop(0).start()
+
+    def spans(self, stage):
+        half = self.blocks >> (stage + 1)
+        start = 0
+        for k in range(stage):
+            start = start + partner_of(self.rest[k])[1] * (self.blocks >> (k + 1))
+        side = partner_of(self.rest[stage])[1]
+        return half, start + side * half, start + (1 - side) * half, self.blocks - 2 * half
+
+    def hop(self, stage):
+        half, _, away, landing = self.spans(stage)
+        return pltpu.make_async_remote_copy(
+            src_ref=self.sums.at[pl.ds(away, half)], dst_ref=self.got.at[pl.ds(landing, half)],
+            send_sem=self.hop_send.at[stage], recv_sem=self.hop_recv.at[stage],
+            device_id={"batch": partner_of(self.rest[stage])[0]}, device_id_type=MESH)
+
+    def advance(self, stage):
+        half, keep, _, landing = self.spans(stage)
+        self.hop(stage).wait_recv()
+        if self.by_rows or stage + 1 < self.stages:
+            if stage + 1 == self.stages:
+                self.out[...] = self.sums[keep].astype(F32) + self.got[landing].astype(F32)
+                return
+
+            def add(j, carry):
+                self.sums[keep + j] = (self.sums[keep + j].astype(F32)
+                                       + self.got[landing + j].astype(F32)).astype(BF16)
+                return carry
+
+            lax.fori_loop(0, half, add, 0)
+            self.hop(stage + 1).start()
+        else:
+            mine, theirs = self.sums[keep].astype(F32), self.got[landing].astype(F32)
+            first = self.side() == 0
+            self.out[:, :self.wide] = jnp.where(first, mine, theirs)
+            self.out[:, self.wide:] = jnp.where(first, theirs, mine)
+
+    def drain(self):
+        for copy in self.operand(1, True):
+            copy.wait_send()
+        for stage in range(self.stages):
+            self.hop(stage).wait_send()
+
+
+class Small:
+    def __init__(self, owner, bits):
+        self.owner, self.bits = owner, bits
+        self.stages = bits
+
+    def scratch(self, dims):
+        dma = pltpu.SemaphoreType.DMA
+        return [pltpu.VMEM((self.bits + 1,) + dims, F32), pltpu.VMEM((self.bits + 1,) + dims, F32),
+                dma((self.bits + 1,)), dma((self.bits + 1,))]
+
+    def bind(self, x, out, scratch):
+        self.x, self.out = x, out
+        self.got, self.sums, self.sent, self.came = scratch
+        return self
+
+    def arrive(self):
+        return pltpu.make_async_remote_copy(
+            src_ref=self.x, dst_ref=self.got.at[self.bits], send_sem=self.sent.at[self.bits],
+            recv_sem=self.came.at[self.bits], device_id={"section": self.owner}, device_id_type=MESH)
+
+    def hop(self, stage):
+        return pltpu.make_async_remote_copy(
+            src_ref=self.sums.at[stage], dst_ref=self.got.at[stage], send_sem=self.sent.at[stage],
+            recv_sem=self.came.at[stage], device_id={"batch": partner_of(stage)[0]},
+            device_id_type=MESH)
+
+    def send_from_owner(self):
+        pass
+
+    def send_from_other(self):
+        self.arrive().start()
+
+    def sent_from_other(self):
+        self.arrive().wait_send()
+
+    def multiply(self):
+        self.arrive().wait_recv()
+        self.sums[0] = self.x[...] + self.got[self.bits]
+        self.hop(0).start()
+
+    def advance(self, stage):
+        self.hop(stage).wait_recv()
+        self.sums[stage + 1] = self.sums[stage] + self.got[stage]
+        if stage + 1 < self.bits:
+            self.hop(stage + 1).start()
+        else:
+            self.out[...] = self.sums[self.bits]
+
+    def drain(self):
+        for stage in range(self.bits):
+            self.hop(stage).wait_send()
+
+
+def greet(owner, bits, near):
+    barrier = pltpu.get_barrier_semaphore()
     mine = lax.axis_index("section") == owner
-    barrier = pltpu.get_barrier_semaphore()
-
-    def operand(i, first):
-        source, target = (xs[i], xr[i]) if first else (ys[i], yr[i])
-        slot = 2 * i + (0 if first else 1)
-        return pltpu.make_async_remote_copy(
-            src_ref=source, dst_ref=target, send_sem=op_send.at[slot], recv_sem=op_recv.at[slot],
-            device_id={"section": owner}, device_id_type=MESH)
-
-    def vec_in():
-        return pltpu.make_async_remote_copy(
-            src_ref=vec_ref, dst_ref=vec_got.at[bits], send_sem=v_send.at[bits],
-            recv_sem=v_recv.at[bits], device_id={"section": owner}, device_id_type=MESH)
-
-    @pl.when(jnp.logical_not(mine))
-    def _():
-        pl.semaphore_wait(barrier, 1)
-        for i in range(count):
-            operand(i, True).start()
-            operand(i, False).start()
-        vec_in().start()
-        for i in range(count):
-            operand(i, True).wait_send()
-            operand(i, False).wait_send()
-        vec_in().wait_send()
 
     @pl.when(mine)
     def _():
@@ -537,74 +701,47 @@
         for bit in range(bits):
             pl.semaphore_signal(
                 barrier, inc=1, device_id={"batch": partner_of(bit)[0]}, device_id_type=MESH)
+        for bit in near:
+            pl.semaphore_signal(
+                barrier, inc=1, device_id={"section": 1 - owner, "batch": partner_of(bit)[0]},
+                device_id_type=MESH)
         pl.semaphore_wait(barrier, bits)
 
-        def spans(i, stage):
-            order = orders[i]
-            half = 1 << (bits - 1 - stage)
-            start = 0
-            for k in range(stage):
-                start = start + partner_of(order[k])[1] * (1 << (bits - 1 - k))
-            side = partner_of(order[stage])[1]
-            landing = (1 << bits) - 2 * half
-            return half, start + side * half, start + (1 - side) * half, landing
-
-        def hop(i, stage):
-            half, _, away, landing = spans(i, stage)
-            return pltpu.make_async_remote_copy(
-                src_ref=grads[i].at[pl.ds(away, half)], dst_ref=got[i].at[pl.ds(landing, half)],
-                send_sem=rs_send.at[i, stage], recv_sem=rs_recv.at[i, stage],
-                device_id={"batch": partner_of(orders[i][stage])[0]}, device_id_type=MESH)
-
-        def vec_hop(stage):
-            return pltpu.make_async_remote_copy(
-                src_ref=vec_sum.at[stage], dst_ref=vec_got.at[stage],
-                send_sem=v_send.at[stage], recv_sem=v_recv.at[stage],
-                device_id={"batch": partner_of(stage)[0]}, device_id_type=MESH)
-
-        vec_in().wait_recv()
-        vec_sum[0] = vec_ref[...] + vec_got[bits]
-        vec_hop(0).start()
-        for i in range(count):
-            operand(i, True).wait_recv()
-            operand(i, False).wait_recv()
-            depth, columns = xs[i].shape[1], ys[i].shape[1]
-            block = grads[i].shape[1]
-            rows = block * 128 // math.gcd(block, 128)
-            step = min(columns, 768)
-            for base in range(0, depth, rows):
-                left = cat([xs[i][:, base:base + rows], xr[i][:, base:base + rows]], 0)
-                for c in range(0, columns, step):
-                    right = cat([ys[i][:, c:c + step], yr[i][:, c:c + step]], 0)
-                    value = tn(left, right).astype(BF16)
-                    for j in range(rows // block):
-                        spot = place_of(base // block + j, orders[i])
-                        grads[i][spot, :, c:c + step] = value[j * block:(j + 1) * block]
-            hop(i, 0).start()
+    @pl.when(jnp.logical_not(mine))
+    def _():
+        pl.semaphore_wait(barrier, 1 + len(near))
+
+
+def reduce_weights(*refs, weights, small):
+    count = len(weights)
+    owner, bits = small.owner, small.bits
+    xs, ys, vec = refs[:count], refs[count:2 * count], refs[2 * count]
+    outs, vec_out = refs[2 * count + 1:3 * count + 1], refs[3 * count + 1]
+    rest = refs[3 * count + 2:]
+    items = [w.bind(xs[i], ys[i], outs[i], rest[8 * i:8 * i + 8]) for i, w in enumerate(weights)]
+    items = [small.bind(vec, vec_out, rest[8 * count:])] + items
+    mine = lax.axis_index("section") == owner
+    greet(owner, bits, sorted({w.order[0] for w in weights}))
+
+    @pl.when(mine)
+    def _():
+        for item in items:
+            item.send_from_owner()
+        for item in items:
+            item.multiply()
         for stage in range(bits):
-            vec_hop(stage).wait_recv()
-            vec_sum[stage + 1] = vec_sum[stage] + vec_got[stage]
-            if stage + 1 < bits:
-                vec_hop(stage + 1).start()
-            for i in range(count):
-                half, keep, _, landing = spans(i, stage)
-                hop(i, stage).wait_recv()
-                if stage + 1 < bits:
-                    def add(j, carry):
-                        grads[i][keep + j] = (
-                            grads[i][keep + j].astype(F32) + got[i][landing + j].astype(F32)
-                        ).astype(BF16)
-                        return carry
-
-                    lax.fori_loop(0, half, add, 0)
-                    hop(i, stage + 1).start()
-                else:
-                    outs[i][...] = grads[i][keep].astype(F32) + got[i][landing].astype(F32)
-        vec_out[...] = vec_sum[bits]
-        for stage in range(bits):
-            vec_hop(stage).wait_send()
-            for i in range(count):
-                hop(i, stage).wait_send()
+            for item in items:
+                if stage < item.stages:
+                    item.advance(stage)
+        for item in items:
+            item.drain()
+
+    @pl.when(jnp.logical_not(mine))
+    def _():
+        for item in items:
+            item.send_from_other()
+        for item in items:
+            item.sent_from_other()
 
 
 def shape(dims, kind=F32):
@@ -689,26 +826,21 @@
         jnp.zeros((16 - sums.shape[0] - 3 - dtaps.size // width, width), F32)], axis=0)
 
 
+def plan(owner, bits):
+    tail = tuple(range(3, bits))
+    return [Weight(owner, (1, 0, 2) + tail, True), Weight(owner, (0, 1, 2) + tail, False),
+            Weight(owner, (1, 0, 2) + tail, False), Weight(owner, (2, 1, 0) + tail, False)]
+
+
 def reduce_on_slice(owner, xs, ys, small, batch):
     bits = batch.bit_length() - 1
-    count = len(xs)
-    first = (0, 1, 2)
-    orders = []
-    for i in (0, 1, 2, 2):
-        turned = [first[i], first[(i + 1) % 3], first[(i + 2) % 3]]
-        orders.append(tuple(turned + list(range(3, bits))))
-    blocks = [x.shape[1] // batch for x in xs]
-    outs = [shape((b, y.shape[1])) for b, y in zip(blocks, ys)] + [shape(small.shape)]
-    scratch = [pltpu.VMEM(x.shape, BF16) for x in xs] + [pltpu.VMEM(y.shape, BF16) for y in ys]
-    scratch += [pltpu.VMEM((batch, b, y.shape[1]), BF16) for b, y in zip(blocks, ys)]
-    scratch += [pltpu.VMEM((batch - 1, b, y.shape[1]), BF16) for b, y in zip(blocks, ys)]
-    scratch += [pltpu.VMEM((bits + 1,) + small.shape, F32), pltpu.VMEM((bits + 1,) + small.shape, F32)]
-    dma = pltpu.SemaphoreType.DMA
-    scratch += [dma((2 * count,)), dma((2 * count,)), dma((count, bits)), dma((count, bits)),
-                dma((bits + 1,)), dma((bits + 1,))]
+    weights = [w.sizes(x.shape, y.shape) for w, x, y in zip(plan(owner, bits), xs, ys)]
+    outs = [shape((w.block, w.width)) for w in weights] + [shape(small.shape)]
+    little = Small(owner, bits)
+    scratch = [s for w in weights for s in w.scratch()] + little.scratch(small.shape)
     return call(
-        functools.partial(reduce_weights, owner=owner, orders=tuple(orders)),
-        "reduce_weights", [IN_VMEM] * (2 * count + 1), outs, scratch,
+        functools.partial(reduce_weights, weights=weights, small=little),
+        "reduce_weights", [IN_VMEM] * (2 * len(xs) + 1), outs, scratch,
         tuple(xs) + tuple(ys) + (small,), 4 * 10 ** 9, 10 ** 7, collective=owner)
 
 

time: 345 us -> 325 us (0.942)
  Pallas kernels: 287 us -> 267 us
    pallas_call x10, Pallas kernels: 287 us -> 267 us  [call(): pl.pallas_call(kernel, out_shape=tuple(outs), in_specs=ins, out_specs=(IN...]
  transfers between devices with their start and end apart: 7 -> 7, of which waited for: 1 -> 1; matrix products, arithmetic and copies ran while one was open for 6% -> 7% of each run, Pallas kernels for 6% -> 7%
where the time goes in v2:
time: 325 us; the launch traced here: 321 us
  Pallas kernels  267 us (82%)
  local copies, waits for them, and re-layouts  27.9 us (9%)
  other arithmetic  13.7 us (4%)
  waiting for transfers between devices  8.8 us (3%)
    pallas_call x10, Pallas kernels, call(): pl.pallas_call(kernel, out_shape=tuple(outs), in_specs=ins, out_specs=(IN...  267 us
    ppermute x7, waiting for transfers between devices, swap(): return lax.ppermute(value, 'section', [(0, 1), (1, 0)])  8.8 us
    dynamic_slice x7, local copies, waits for them, and re-layouts, share(): return lax.dynamic_slice_in_dim(flat, index * size, size, 0)[None]  8.2 us
  transfers between devices with their start and end apart: 7, of which 1 were waited for; matrix products, arithmetic and copies ran while one was open for 7% of the time, Pallas kernels for 7%

profile of v2, /device:TPU:0, one launch (start us, length us, event | category | flops | bytes accessed | tf_op | source)
XLA Modules:
  0.0 320.7 jit_solution(7838400625395890121)
XLA Ops:
  3.6 1.4 reduce.4
  5.0 1.5 concatenate.61
  9.0 1.6 constant_dynamic-slice_fusion.6.g_ref
  13.8 8.8 %collective-permute-done.1.other_ref = bf16[768,2304]{1,0:T(8,128)(2,1)} collective-permute-done((bf16[768,2304]{1,0:T(8,128)(2,1)}, bf16[768,2304]{1,0:T(8,128)(2,1)}, u32[]{:S(2)}, u32[]{:S(2)}) %collective-permute-start.1) | collective-permute-done | bytes 3538976 | tf_op jit(solution)/shard_map/ppermute | solution.py:848
  22.6 22.1 %attention_forward.2 = (bf16[128,768]{1,0:T(8,128)(2,1)}, bf16[3,128,768]{2,1,0:T(8,128)(2,1)}, bf16[2,64,768]{2,1,0:T(8,128)(2,1)}, f32[128,768]{1,0:T(8,128)},...) custom-call(s32[2]{0:T(128)} %get-tuple-element.164.sel_ref, ...), custom_call_target="tpu_custom_call" | custom-call | flops 10000000000 | bytes 10000000 | tf_op jit(solution)/shard_map/attention_forward/pallas_call | solution.py:759
  46.7 7.3 %post_forward.2 = (bf16[128,768]{1,0:T(8,128)(2,1)}, bf16[128,768]{1,0:T(8,128)(2,1)}, bf16[128,3072]{1,0:T(8,128)(2,1)}, f32[128,768]{1,0:T(8,128)}, f32[128,76...) custom-call(s32[2]{0:T(128)} %get-tuple-element.164.sel_ref, ...), custom_call_target="tpu_custom_call" | custom-call | flops 2000000000 | bytes 10000000 | tf_op jit(solution)/shard_map/post_forward/pallas_call | solution.py:759
  54.0 21.8 %attention_forward.3 = (bf16[128,768]{1,0:T(8,128)(2,1)}, bf16[3,128,768]{2,1,0:T(8,128)(2,1)}, bf16[2,64,768]{2,1,0:T(8,128)(2,1)}, f32[128,768]{1,0:T(8,128)},...) custom-call(s32[2]{0:T(128)} %get-tuple-element.165.sel_ref, ...), custom_call_target="tpu_custom_call" | custom-call | flops 10000000000 | bytes 10000000 | tf_op jit(solution)/shard_map/attention_forward/pallas_call | solution.py:759
  76.7 7.4 %post_forward.3 = (bf16[128,768]{1,0:T(8,128)(2,1)}, bf16[128,768]{1,0:T(8,128)(2,1)}, bf16[128,3072]{1,0:T(8,128)(2,1)}, f32[128,768]{1,0:T(8,128)}, f32[128,76...) custom-call(s32[2]{0:T(128)} %get-tuple-element.165.sel_ref, ...), custom_call_target="tpu_custom_call" | custom-call | flops 2000000000 | bytes 10000000 | tf_op jit(solution)/shard_map/post_forward/pallas_call | solution.py:759
  84.1 9.1 %post_backward.2 = (bf16[128,768]{1,0:T(8,128)(2,1)}, bf16[128,3072]{1,0:T(8,128)(2,1)}, bf16[128,768]{1,0:T(8,128)(2,1)}, f32[128,768]{1,0:T(8,128)}, f32[128,768]{1,0:T(8,128)}, /*index=5*/f32[10,768]{1,0:T(8,128)}) custom-call(s32[2]{0:T(128)} %get-tuple-element.165.sel_ref, bf16[128,768]{1,0:T(8,128)(2,1)} %constant_dynamic-slice_fusion.6.g_ref, ...), custom_call_target="tpu_custom_call" | custom-call | flops 2000000000 | bytes 10000000 | tf_op jit(solution)/shard_map/post_backward/pallas_call | solution.py:759
  93.3 20.1 %attention_backward.2 = (bf16[128,2304]{1,0:T(8,128)(2,1)}, bf16[128,768]{1,0:T(8,128)(2,1)}, f32[3,768]{1,0:T(4,128)}, f32[16,128]{1,0:T(8,128)}) custom-call(s32[2]{0:T(128)} %get-tuple-element.165.sel_ref, f32[128,768]{1,0:T(8,128)} %get-tuple-element.88.do_ref, f32[128,768]{1,0:T(8,128)} %get-tuple-element.89.gr_ref, ...), custom_call_target="tpu_custom_call" | custom-call | flops 10000000000 | bytes 10000000 | tf_op jit(solution)/shard_map/attention_backward/pallas_call | solution.py:759
  114.1 9.1 %post_backward.3 = (bf16[128,768]{1,0:T(8,128)(2,1)}, bf16[128,3072]{1,0:T(8,128)(2,1)}, bf16[128,768]{1,0:T(8,128)(2,1)}, f32[128,768]{1,0:T(8,128)}, f32[128,768]{1,0:T(8,128)}, /*index=5*/f32[10,768]{1,0:T(8,128)}) custom-call(s32[2]{0:T(128)} %get-tuple-element.164.sel_ref, bf16[128,768]{1,0:T(8,128)(2,1)} %get-tuple-element.98.g_ref, ...), custom_call_target="tpu_custom_call" | custom-call | flops 2000000000 | bytes 10000000 | tf_op jit(solution)/shard_map/post_backward/pallas_call | solution.py:759
  123.2 19.9 %attention_backward.3 = (bf16[128,2304]{1,0:T(8,128)(2,1)}, bf16[128,768]{1,0:T(8,128)(2,1)}, f32[3,768]{1,0:T(4,128)}, f32[16,128]{1,0:T(8,128)}) custom-call(s32[2]{0:T(128)} %get-tuple-element.164.sel_ref, f32[128,768]{1,0:T(8,128)} %get-tuple-element.103.do_ref, f32[128,768]{1,0:T(8,128)} %get-tuple-element.104.gr_ref, ...), custom_call_target="tpu_custom_call" | custom-call | flops 10000000000 | bytes 10000000 | tf_op jit(solution)/shard_map/attention_backward/pallas_call | solution.py:759
  144.7 2.0 concatenate.73.refs_8_
  146.7 2.0 concatenate.72.refs_8_
  148.7 30.5 %reduce_weights.3 = (f32[192,768]{1,0:T(8,128)}, f32[48,3072]{1,0:T(8,128)}, f32[48,2304]{1,0:T(8,128)}, f32[48,768]{1,0:T(8,128)}, f32[16,768]{1,0:T(8,128)}) custom-call(bf16[128,3072]{1,0:T(8,128)(2,1)} %get-tuple-element.125.refs_0_, bf16[128,768]{1,0:T(8,128)(2,1)} %get-tuple-element.126.refs_1_, bf16[128,768]{1,0:T(8,128)(2,1)} %get-tuple-element.81.x_ref.refs_2_, ...), custom_call_target="tpu_custom_call" | custom-call | flops 4000000000 | bytes 10000000 | tf_op jit(solution)/shard_map/reduce_weights/pallas_call | solution.py:759
  179.2 119.1 %reduce_weights.2 = (f32[192,768]{1,0:T(8,128)}, f32[48,3072]{1,0:T(8,128)}, f32[48,2304]{1,0:T(8,128)}, f32[48,768]{1,0:T(8,128)}, f32[16,768]{1,0:T(8,128)}) custom-call(bf16[128,3072]{1,0:T(8,128)(2,1)} %get-tuple-element.114.refs_0_, bf16[128,768]{1,0:T(8,128)(2,1)} %get-tuple-element.115.refs_1_, ...), custom_call_target="tpu_custom_call" | custom-call | flops 4000000000 | bytes 10000000 | tf_op jit(solution)/shard_map/reduce_weights/pallas_call | solution.py:759
  301.7 1.3 constant_dynamic-slice_fusion
  302.9 1.3 constant_dynamic-slice_fusion.1
  304.2 1.3 constant_dynamic-slice_fusion.2
  305.4 1.2 constant_dynamic-slice_fusion.3
  306.7 1.3 constant_dynamic-slice_fusion.4
  310.6 2.0 select_bitcast_fusion
  312.6 2.0 select_bitcast_fusion.1
  316.0 1.3 dynamic_slice.41
  (96 shorter events, 23.8 us)
Async XLA Ops:
  0.6 7.7 %copy-start = (bf16[256,768]{1,0:T(8,128)(2,1)S(1)}, bf16[256,768]{1,0:T(8,128)(2,1)}, u32[]{:S(2)}) copy-start(bf16[256,768]{1,0:T(8,128)(2,1)} %param.16) | copy-start | bytes 1179652
  0.7 45.0 %collective-permute-start.3 = (bf16[768,3072]{1,0:T(8,128)(2,1)}, bf16[768,3072]{1,0:T(8,128)(2,1)}, u32[]{:S(2)}, u32[]{:S(2)}) collective-permute-start(bf16[768,3072]{1,0:T(8,128)(2,1)} %bitcast.29), channel_id=1, source_target_pairs={{0,16},{16,0},{1,17},{17,1},{2,18},{18,2},{3,19},{19,3},{4,20},{20... | collective-permute-start | bytes 14155784 | tf_op jit(solution)/shard_map/ppermute | solution.py:848
  1.2 44.5 %collective-permute-start.4 = (bf16[3072,768]{1,0:T(8,128)(2,1)}, bf16[3072,768]{1,0:T(8,128)(2,1)}, u32[]{:S(2)}, u32[]{:S(2)}) collective-permute-start(bf16[3072,768]{1,0:T(8,128)(2,1)} %bitcast.34), channel_id=1, source_target_pairs={{0,16},{16,0},{1,17},{17,1},{2,18},{18,2},{3,19},{19,3},{4,20},{20... | collective-permute-start | bytes 14155784 | tf_op jit(solution)/shard_map/ppermute | solution.py:848
  1.3 21.4 %collective-permute-start.1 = (bf16[768,2304]{1,0:T(8,128)(2,1)}, bf16[768,2304]{1,0:T(8,128)(2,1)}, u32[]{:S(2)}, u32[]{:S(2)}) collective-permute-start(bf16[768,2304]{1,0:T(8,128)(2,1)} %bitcast.55), channel_id=1, source_target_pairs={{0,16},{16,0},{1,17},{17,1},{2,18},{18,2},{3,19},{19,3},{4,20},{20... | collective-permute-start | bytes 10616840 | tf_op jit(solution)/shard_map/ppermute | solution.py:848
  6.5 5.4 %collective-permute-start = (f32[14,768]{1,0:T(8,128)S(1)}, f32[14,768]{1,0:T(8,128)S(1)}, u32[]{:S(2)}, u32[]{:S(2)}) collective-permute-start(f32[14,768]{1,0:T(8,128)S(1)} %concatenate.61), channel_id=1, source_target_pairs={{0,16},{16,0},{1,17},{17,1},{2,18},{18,2},{3,19},{19,3},{4,20},{20... | collective-permute-start | bytes 129032 | tf_op jit(solution)/shard_map/ppermute | solution.py:848
  6.7 39.0 %collective-permute-start.2 = (bf16[768,768]{1,0:T(8,128)(2,1)}, bf16[768,768]{1,0:T(8,128)(2,1)S(1)}, u32[]{:S(2)}, u32[]{:S(2)}) collective-permute-start(bf16[768,768]{1,0:T(8,128)(2,1)} %bitcast.39), channel_id=1, source_target_pairs={{0,16},{16,0},{1,17},{17,1},{2,18},{18,2},{3,19},{19,3},{4,20},{20... | collective-permute-start | bytes 3538952 | tf_op jit(solution)/shard_map/ppermute | solution.py:848
  11.9 32.9 %copy-start.8 = (f32[14,768]{1,0:T(8,128)}, f32[14,768]{1,0:T(8,128)S(1)}, u32[]{:S(2)}) copy-start(f32[14,768]{1,0:T(8,128)S(1)} %get-tuple-element.145.vec_ref) | copy-start | bytes 129028
  11.9 32.9 %copy-start.9 = (f32[14,768]{1,0:T(8,128)}, f32[14,768]{1,0:T(8,128)S(1)}, u32[]{:S(2)}) copy-start(f32[14,768]{1,0:T(8,128)S(1)} %get-tuple-element.144.vec_ref) | copy-start | bytes 129028
  123.2 20.7 %copy-start.17 = (f32[3,768]{1,0:T(4,128)S(1)}, f32[3,768]{1,0:T(4,128)}, u32[]{:S(2)}) copy-start(f32[3,768]{1,0:T(4,128)} %get-tuple-element.132) | copy-start | bytes 27652
  123.2 21.5 %copy-start.14 = (f32[10,768]{1,0:T(8,128)S(1)}, f32[10,768]{1,0:T(8,128)}, u32[]{:S(2)}) copy-start(f32[10,768]{1,0:T(8,128)} %get-tuple-element.131) | copy-start | bytes 92164
  123.2 23.5 %copy-start.15 = (f32[10,768]{1,0:T(8,128)S(1)}, f32[10,768]{1,0:T(8,128)}, u32[]{:S(2)}) copy-start(f32[10,768]{1,0:T(8,128)} %get-tuple-element.120) | copy-start | bytes 92164
  179.1 119.3 %copy-start.16 = (f32[16,768]{1,0:T(8,128)S(1)}, f32[16,768]{1,0:T(8,128)}, u32[]{:S(2)}) copy-start(f32[16,768]{1,0:T(8,128)} %get-tuple-element.137) | copy-start | bytes 147460
  179.2 130.8 %copy-start.3 = (bf16[128,768]{1,0:T(8,128)(2,1)S(1)}, bf16[128,768]{1,0:T(8,128)(2,1)}, u32[]{:S(2)}) copy-start(bf16[128,768]{1,0:T(8,128)(2,1)} %get-tuple-element.98.g_ref) | copy-start | bytes 589828
  179.2 130.8 %copy-start.5 = (bf16[128,768]{1,0:T(8,128)(2,1)S(1)}, bf16[128,768]{1,0:T(8,128)(2,1)}, u32[]{:S(2)}) copy-start(bf16[128,768]{1,0:T(8,128)(2,1)} %get-tuple-element.113) | copy-start | bytes 589828
  179.2 130.8 %copy-start.2 = (bf16[128,768]{1,0:T(8,128)(2,1)S(1)}, bf16[128,768]{1,0:T(8,128)(2,1)}, u32[]{:S(2)}) copy-start(bf16[128,768]{1,0:T(8,128)(2,1)} %get-tuple-element.81.x_ref.refs_2_) | copy-start | bytes 589828
  179.2 130.8 %copy-start.4 = (bf16[128,768]{1,0:T(8,128)(2,1)S(1)}, bf16[128,768]{1,0:T(8,128)(2,1)}, u32[]{:S(2)}) copy-start(bf16[128,768]{1,0:T(8,128)(2,1)} %get-tuple-element.83) | copy-start | bytes 589828
  179.2 131.4 %copy-start.7 = (f32[192,768]{1,0:T(8,128)S(1)}, f32[192,768]{1,0:T(8,128)}, u32[]{:S(2)}) copy-start(f32[192,768]{1,0:T(8,128)} %get-tuple-element.143) | copy-start | bytes 1769476
  179.2 133.4 %copy-start.6 = (f32[48,3072]{1,0:T(8,128)S(1)}, f32[48,3072]{1,0:T(8,128)}, u32[]{:S(2)}) copy-start(f32[48,3072]{1,0:T(8,128)} %get-tuple-element.141) | copy-start | bytes 1769476
  298.4 16.2 %copy-start.12 = (f32[48,768]{1,0:T(8,128)S(1)}, f32[48,768]{1,0:T(8,128)}, u32[]{:S(2)}) copy-start(f32[48,768]{1,0:T(8,128)} %get-tuple-element.139) | copy-start | bytes 442372
  298.4 16.2 %copy-start.13 = (f32[48,768]{1,0:T(8,128)S(1)}, f32[48,768]{1,0:T(8,128)}, u32[]{:S(2)}) copy-start(f32[48,768]{1,0:T(8,128)} %get-tuple-element.138) | copy-start | bytes 442372
  298.4 16.8 %copy-start.10 = (f32[48,2304]{1,0:T(8,128)S(1)}, f32[48,2304]{1,0:T(8,128)}, u32[]{:S(2)}) copy-start(f32[48,2304]{1,0:T(8,128)} %get-tuple-element.135) | copy-start | bytes 1327108
  298.4 16.8 %copy-start.11 = (f32[48,2304]{1,0:T(8,128)S(1)}, f32[48,2304]{1,0:T(8,128)}, u32[]{:S(2)}) copy-start(f32[48,2304]{1,0:T(8,128)} %get-tuple-element.124) | copy-start | bytes 1327108
  310.0 8.5 %collective-permute-start.5 = (bf16[128,768]{1,0:T(8,128)(2,1)S(1)}, bf16[128,768]{1,0:T(8,128)(2,1)S(1)}, u32[]{:S(2)}, u32[]{:S(2)}) collective-permute-start(bf16[128,768]{1,0:T(8,128)(2,1)S(1)} %broadcast_select_fusion.1), channel_id=1, source_target_pairs={{0,16},{16,0},{1,17},{17,1},{2,18},{18,2},{3,19},{19,3},{4,20},{20... | collective-permute-start | bytes 589832 | tf_op jit(solution)/shard_map/ppermute | solution.py:848
  310.1 9.3 %collective-permute-start.6 = (bf16[128,768]{1,0:T(8,128)(2,1)S(1)}, bf16[128,768]{1,0:T(8,128)(2,1)S(1)}, u32[]{:S(2)}, u32[]{:S(2)}) collective-permute-start(bf16[128,768]{1,0:T(8,128)(2,1)S(1)} %broadcast_select_fusion), channel_id=1, source_target_pairs={{0,16},{16,0},{1,17},{17,1},{2,18},{18,2},{3,19},{19,3},{4,20},{20... | collective-permute-start | bytes 589832 | tf_op jit(solution)/shard_map/ppermute | solution.py:848
  (1 other events, 1.0 us)

commit v3 on v2

--- a/solution.py
+++ b/solution.py
@@ -139,10 +139,6 @@
     pool = pool_matrix(length, rows)
     eye = pair_eye()
     sl = [pl.ds(p * PAIR, PAIR) for p in range(pairs)]
-    for p in range(pairs):
-        for j in range(2):
-            t_ref[p, :, j * rows:(j + 1) * rows] = toeplitz(
-                taps_ref[2 * p + j:2 * p + j + 1, :], rows, taps)
     valid = (lax.broadcasted_iota(jnp.int32, (rows, width), 0) < length).astype(F32)
     scale = LM ** (-0.25)
     x = x_ref[...]
@@ -221,143 +217,15 @@
         db_ref[1, :, sl[p]] = bs[0]
         a1 = pair_softmax(nt3(qs[p], kld[p]), ones)
         a1_ref[:, sl[p]] = a1
-        th, tl = split(t_ref[p])
+        band = cat([toeplitz(taps_ref[2 * p + j:2 * p + j + 1, :], rows, taps) for j in range(2)], 1)
+        th, tl = split(band)
+        t_ref[p] = th
         o = nn3(split(a1), bs) + nn(cat([th, tl], 1), cat([vh, vh], 0)) + nn(th, vl)
         att_ref[:, sl[p]] = o.astype(BF16)
 
 
 def softmax_back(a, da, ones):
     return a * (da - half_sums(a * da, ones))
-
-
-def attention_backward(
-    sel_ref, do_ref, gr_ref, qkv_ref, lm_ref, a1_ref, a2_ref, a3_ref, t_ref, newton_ref, db_ref,
-    own_ref, other_ref,
-    dqkv_ref, gi_ref, col_ref, dtaps_ref,
-    w_ref, dz_ref, dr_ref, da_ref, sem, *, taps):
-    rows, width = do_ref.shape
-    pairs = width // PAIR
-    length = sel_ref[1]
-
-    def part(i, source):
-        return pltpu.make_async_copy(source.at[:, pl.ds(i * width, width)], w_ref.at[i], sem.at[i])
-
-    @pl.when(sel_ref[0] == 1)
-    def _():
-        for i in range(3):
-            part(i, own_ref).start()
-
-    @pl.when(sel_ref[0] == 0)
-    def _():
-        for i in range(3):
-            part(i, other_ref).start()
-
-    ones = block_ones()
-    eye = pair_eye()
-    pool = pool_matrix(length, rows)
-    sl = [pl.ds(p * PAIR, PAIR) for p in range(pairs)]
-    doh = [do_ref[:, sl[p]].astype(BF16) for p in range(pairs)]
-    ddh = []
-    for p in range(pairs):
-        a1 = a1_ref[:, sl[p]].astype(BF16)
-        db = pick(tn(a1, doh[p]))
-        dbh = db.astype(BF16)
-        z = newton_ref[0, NEWTON, :, sl[p]].astype(BF16)
-        dz_ref[:, sl[p]] = nt(dbh, spread(db_ref[0, :, sl[p]]))
-        dr_ref[:, sl[p]] = jnp.zeros((LM, PAIR), F32)
-        ddh.append(pick(tn(z, dbh)).astype(BF16))
-
-    def newton_back(index, carry):
-        step = NEWTON - 1 - index
-        keep = []
-        for p in range(pairs):
-            z = newton_ref[0, step, :, sl[p]]
-            zh, zl = split(z)
-            dz = dz_ref[:, sl[p]]
-            gh, gl = split(dz)
-            full = tn(cat([zh, zh, zl], 0), cat([gh, gl, gh], 0))
-            df = pick(full + full.T) * 0.5
-            keep.append((df, (gh, gl)))
-        for p in range(pairs):
-            df, g = keep[p]
-            r, s, t = [newton_ref[i, step, :, sl[p]] for i in (1, 2, 3)]
-            dz_ref[:, sl[p]] = nn3(g, split(eye + r + s + 0.25 * t))
-            dr = dr_ref[:, sl[p]]
-            dt = 0.25 * df + 0.75 * dr
-            rs, ss, dts, drs = split(r), split(s), split(dt), split(0.5 * dr)
-            m = nn3(dts, rs) + nn3(drs, ss)
-            keep[p] = (df, dts, m, rs, ss)
-        for p in range(pairs):
-            df, dts, m, rs, ss = keep[p]
-            ds = 2.0 * df + (m + pair_transpose(m))
-            m = nn3(dts, ss) + nn3(split(ds), rs)
-            dr_ref[:, sl[p]] = df + 0.5 * (m + pair_transpose(m))
-        return carry
-
-    lax.fori_loop(0, NEWTON, newton_back, 0)
-    first = lane_is_first(1)
-    for p in range(pairs):
-        a = a2_ref[:, sl[p]]
-        at = pair_transpose(a)
-        dz = dz_ref[:, sl[p]]
-        g = nn3(split(dr_ref[:, sl[p]]), split(a))
-
-        def halves(m):
-            c = jnp.sum(m, axis=0, keepdims=True)
-            ca = jnp.sum(jnp.where(first, c, 0.0), axis=1, keepdims=True)
-            cb = jnp.sum(jnp.where(first, 0.0, c), axis=1, keepdims=True)
-            return jnp.where(first, ca, cb)
-
-        inv = 1.0 / halves(a * a)
-        dc = halves(dz * at) - halves(g * a)
-        da_ref[:, sl[p]] = inv * (pair_transpose(dz) - 2.0 * g) - (2.0 * dc * inv * inv) * a
-    scale = LM ** (-0.25)
-    valid = (lax.broadcasted_iota(jnp.int32, (rows, PAIR), 0) < length).astype(F32)
-    half = taps // 2
-    row = lax.broadcasted_iota(jnp.int32, (rows, rows), 0)
-    col = lax.broadcasted_iota(jnp.int32, (rows, rows), 1)
-    flip = (row + col == rows - 1).astype(F32).astype(BF16)
-    near = (col + row <= rows - 1 + half) & (col + row >= rows - 1 - half)
-    for p in range(pairs):
-        q, k, v = [qkv_ref[i, :, sl[p]] for i in range(3)]
-        ql, kl = lm_ref[0, :, sl[p]], lm_ref[1, :, sl[p]]
-        kld, kd, vd = spread(kl), spread(k), spread(v)
-        wide = slice(p * 2 * rows, (p + 1) * 2 * rows)
-        ds2 = softmax_back(a2_ref[:, sl[p]], da_ref[:, sl[p]], ones).astype(BF16)
-        a1 = a1_ref[:, sl[p]]
-        da1 = nt(doh[p], spread(db_ref[1, :, sl[p]]))
-        ds1 = softmax_back(a1, da1, ones).astype(BF16)
-        a3 = a3_ref[:, wide]
-        da3 = nt(ddh[p], vd)
-        parts = []
-        for j in range(2):
-            a, d = a3[:, j * rows:(j + 1) * rows], da3[:, j * rows:(j + 1) * rows]
-            parts.append(a * (d - jnp.sum(a * d, axis=1, keepdims=True)))
-        ds3 = cat(parts, 1).astype(BF16)
-        th = t_ref[p].astype(BF16)
-        dv = pick(tn(cat([a3.astype(BF16), th], 0), cat([ddh[p], doh[p]], 0)))
-        full = nt(spread(nn(flip, doh[p]).astype(BF16)), v)
-        for j in range(2):
-            m = jnp.where(near, full[j * rows:(j + 1) * rows], 0.0)
-            m = pltpu.roll(m, half + 1, 1, stride=1, stride_axis=0)
-            dtaps_ref[2 * p + j:2 * p + j + 1, :] = jnp.sum(m, axis=0, keepdims=True)
-        dkl = pick(tn(cat([ds1, ds2], 0), cat([q, ql], 0)))
-        dql = nn(cat([ds2, ds3], 1), cat([kld, kd], 0))
-        dqlh, dqll = split(dql)
-        dklh, dkll = split(dkl)
-        dq = nn(ds1, kld) + (tn(pool, dqlh) + tn(pool, dqll))
-        dk = pick(tn(ds3, ql)) + (tn(pool, dklh) + tn(pool, dkll))
-        for i, m in enumerate((dq * scale, dk * scale, dv)):
-            low = (m * valid).astype(BF16)
-            dqkv_ref[:, pl.ds(i * width + p * PAIR, PAIR)] = low
-    for i in range(3):
-        col_ref[i:i + 1, :] = jnp.sum(
-            dqkv_ref[:, i * width:(i + 1) * width].astype(F32), axis=0, keepdims=True)
-    total = gr_ref[...]
-    for i in range(3):
-        part(i, own_ref).wait()
-        total = total + nt(dqkv_ref[:, i * width:(i + 1) * width], w_ref[i])
-    gi_ref[...] = total.astype(BF16)
 
 
 def weight_copies(groups, own_refs, other_refs, buffers, sem, flag):
@@ -433,55 +301,6 @@
     y_ref[...] = jnp.where(valid, hat * row(8) + row(9), 0.0).astype(BF16)
 
 
-def post_backward(
-    sel_ref, g_ref, hat1_ref, hat2_ref, rstd_ref, slope_ref, vec_ref,
-    wo_own, we_own, wr_own, wo_oth, we_oth, wr_oth,
-    gd_ref, gu_ref, gp_ref, gr_ref, do_ref, sums_ref,
-    wo_ref, we_ref, wr_ref, sem):
-    rows, width = g_ref.shape
-    chunks = gu_ref.shape[1] // width
-    every = pl.ds(0, width)
-    piece = [pl.ds(c * width, width) for c in range(chunks)]
-    groups = []
-    for c in range(chunks):
-        groups += [(2, piece[c], every), (1, every, piece[c])]
-    groups.append((0, every, every))
-    wait = weight_copies(groups, (wo_own, we_own, wr_own), (wo_oth, we_oth, wr_oth),
-                         (wo_ref, we_ref, wr_ref), sem, sel_ref[0])
-    row = lambda i: vec_ref[i:i + 1, :]
-
-    def total(i, values):
-        sums_ref[i:i + 1, :] = jnp.sum(values, axis=0, keepdims=True)
-
-    valid = lax.broadcasted_iota(jnp.int32, (rows, width), 0) < sel_ref[1]
-    g = jnp.where(valid, g_ref[...].astype(F32), 0.0)
-    hat2 = hat2_ref[...]
-    total(8, g * hat2)
-    total(9, g)
-    second = norm_back(g * row(8), hat2, rstd_ref[:, 1:2])
-    gd = second.astype(BF16)
-    gd_ref[...] = gd
-    total(7, gd.astype(F32))
-    grad = second
-    for c in range(chunks):
-        wait(2 * c)
-        gu = (nt(gd, wr_ref[piece[c], :]) * slope_ref[:, piece[c]]).astype(BF16)
-        gu_ref[:, piece[c]] = gu
-        total(3 + c, gu.astype(F32))
-        wait(2 * c + 1)
-        grad = grad + nt(gu, we_ref[:, piece[c]])
-    hat1 = hat1_ref[...]
-    total(1, grad * hat1)
-    total(2, grad)
-    residual = norm_back(grad * row(1), hat1, rstd_ref[:, 0:1])
-    gr_ref[...] = residual
-    gp = residual.astype(BF16)
-    gp_ref[...] = gp
-    total(0, gp.astype(F32))
-    wait(2 * chunks)
-    do_ref[...] = nt(gp, wo_ref[...])
-
-
 def partner_of(bit):
     me = lax.axis_index("batch")
     side = (me // (1 << bit)) % 2
@@ -517,7 +336,7 @@
             pltpu.VMEM((3, self.rows, self.deep), BF16), pltpu.VMEM((3, self.rows, self.wide), BF16),
             pltpu.VMEM((self.blocks, self.block, self.wide), BF16),
             pltpu.VMEM((self.blocks - 1 if self.by_rows else self.blocks - 1, self.block, self.wide), BF16),
-            dma((2, self.runs + 1)), dma((3, self.runs + 1)), dma((self.stages,)), dma((self.stages,))]
+            dma((3, self.runs + 1)), dma((3, self.runs + 1)), dma((self.stages,)), dma((self.stages,))]
 
     def bind(self, x, y, out, scratch):
         self.x, self.y, self.out = x, y, out
@@ -547,7 +366,7 @@
             for source, lanes in self.pieces(ref, side, first):
                 yield pltpu.make_async_remote_copy(
                     src_ref=source, dst_ref=into.at[slot, :, lanes],
-                    send_sem=self.op_send.at[1 if away else 0, k], recv_sem=self.op_recv.at[slot, k],
+                    send_sem=self.op_send.at[(0, 2, 1)[slot], k], recv_sem=self.op_recv.at[slot, k],
                     device_id=target, device_id_type=MESH)
                 k += 1
 
@@ -691,57 +510,406 @@
             self.hop(stage).wait_send()
 
 
-def greet(owner, bits, near):
+class Stream:
+    def __init__(self, groups, slots, own_refs, other_refs, ring, sem):
+        self.groups, self.slots = groups, slots
+        self.own, self.other, self.ring, self.sem = own_refs, other_refs, ring, sem
+
+    def copy(self, i, refs):
+        _, w, row, col = self.groups[i]
+        size = self.ring.shape[1]
+        source = refs[w].at[pl.ds(row * size, size), pl.ds(col * size, size)]
+        slot = i % self.slots
+        return pltpu.make_async_copy(source, self.ring.at[slot], self.sem.at[slot])
+
+    def start(self, i):
+        if i >= len(self.groups):
+            return
+        own = lax.axis_index("section") == self.groups[i][0]
+
+        @pl.when(own)
+        def _():
+            self.copy(i, self.own).start()
+
+        @pl.when(jnp.logical_not(own))
+        def _():
+            self.copy(i, self.other).start()
+
+    def begin(self):
+        for i in range(self.slots):
+            self.start(i)
+
+    def take(self, i):
+        self.copy(i, self.own).wait()
+        return self.ring[i % self.slots]
+
+    def release(self, i):
+        self.start(i + self.slots)
+
+
+def softmax_back(a, da, ones):
+    return a * (da - half_sums(a * da, ones))
+
+
+def attention_backward(
+    length, do_ref, gr_ref, kept, newton_ref, newton_copy, dqkv_ref, gi_ref, small_ref, at,
+    work, stream, first_group, hook, taps):
+    qkv_ref, lm_ref, a1_ref, a2_ref, a3_ref, t_ref, db_ref = kept
+    dz_ref, dr_ref, da_ref = work
+    rows, width = do_ref.shape
+    pairs = width // PAIR
+    ones = block_ones()
+    eye = pair_eye()
+    pool = pool_matrix(length, rows)
+    sl = [pl.ds(p * PAIR, PAIR) for p in range(pairs)]
+    doh = [do_ref[:, sl[p]].astype(BF16) for p in range(pairs)]
+    newton_copy.wait()
+    ddh = []
+    for p in range(pairs):
+        a1 = a1_ref[:, sl[p]].astype(BF16)
+        db = pick(tn(a1, doh[p]))
+        dbh = db.astype(BF16)
+        z = newton_ref[0, NEWTON, :, sl[p]].astype(BF16)
+        dz_ref[:, sl[p]] = nt(dbh, spread(db_ref[0, :, sl[p]]))
+        dr_ref[:, sl[p]] = jnp.zeros((LM, PAIR), F32)
+        ddh.append(pick(tn(z, dbh)).astype(BF16))
+    hook(0)
+
+    def newton_back(index, carry):
+        step = NEWTON - 1 - index
+        keep = []
+        for p in range(pairs):
+            z = newton_ref[0, step, :, sl[p]]
+            zh, zl = split(z)
+            dz = dz_ref[:, sl[p]]
+            gh, gl = split(dz)
+            full = tn(cat([zh, zh, zl], 0), cat([gh, gl, gh], 0))
+            df = pick(full + full.T) * 0.5
+            keep.append((df, (gh, gl)))
+        for p in range(pairs):
+            df, g = keep[p]
+            r, s, t = [newton_ref[i, step, :, sl[p]] for i in (1, 2, 3)]
+            dz_ref[:, sl[p]] = nn3(g, split(eye + r + s + 0.25 * t))
+            dr = dr_ref[:, sl[p]]
+            dt = 0.25 * df + 0.75 * dr
+            rs, ss, dts, drs = split(r), split(s), split(dt), split(0.5 * dr)
+            m = nn3(dts, rs) + nn3(drs, ss)
+            keep[p] = (df, dts, m, rs, ss)
+        for p in range(pairs):
+            df, dts, m, rs, ss = keep[p]
+            ds = 2.0 * df + (m + pair_transpose(m))
+            m = nn3(dts, ss) + nn3(split(ds), rs)
+            dr_ref[:, sl[p]] = df + 0.5 * (m + pair_transpose(m))
+        return carry
+
+    for half in range(2):
+        lax.fori_loop(half * NEWTON // 2, (half + 1) * NEWTON // 2, newton_back, 0)
+        hook(1 + half)
+    first = lane_is_first(1)
+    for p in range(pairs):
+        a = a2_ref[:, sl[p]]
+        at_ = pair_transpose(a)
+        dz = dz_ref[:, sl[p]]
+        g = nn3(split(dr_ref[:, sl[p]]), split(a))
+
+        def halves(m):
+            c = jnp.sum(m, axis=0, keepdims=True)
+            ca = jnp.sum(jnp.where(first, c, 0.0), axis=1, keepdims=True)
+            cb = jnp.sum(jnp.where(first, 0.0, c), axis=1, keepdims=True)
+            return jnp.where(first, ca, cb)
+
+        inv = 1.0 / halves(a * a)
+        dc = halves(dz * at_) - halves(g * a)
+        da_ref[:, sl[p]] = inv * (pair_transpose(dz) - 2.0 * g) - (2.0 * dc * inv * inv) * a
+    scale = LM ** (-0.25)
+    valid = (lax.broadcasted_iota(jnp.int32, (rows, PAIR), 0) < length).astype(F32)
+    half = taps // 2
+    row = lax.broadcasted_iota(jnp.int32, (rows, rows), 0)
+    col = lax.broadcasted_iota(jnp.int32, (rows, rows), 1)
+    flip = (row + col == rows - 1).astype(F32).astype(BF16)
+    near = (col + row <= rows - 1 + half) & (col + row >= rows - 1 - half)
+    per_row = width // rows
+    for p in range(pairs):
+        q, k, v = [qkv_ref[i, :, sl[p]] for i in range(3)]
+        ql, kl = lm_ref[0, :, sl[p]], lm_ref[1, :, sl[p]]
+        kld, kd, vd = spread(kl), spread(k), spread(v)
+        wide = slice(p * 2 * rows, (p + 1) * 2 * rows)
+        ds2 = softmax_back(a2_ref[:, sl[p]], da_ref[:, sl[p]], ones).astype(BF16)
+        a1 = a1_ref[:, sl[p]]
+        da1 = nt(doh[p], spread(db_ref[1, :, sl[p]]))
+        ds1 = softmax_back(a1, da1, ones).astype(BF16)
+        a3 = a3_ref[:, wide]
+        da3 = nt(ddh[p], vd)
+        parts = []
+        for j in range(2):
+            a, d = a3[:, j * rows:(j + 1) * rows], da3[:, j * rows:(j + 1) * rows]
+            parts.append(a * (d - jnp.sum(a * d, axis=1, keepdims=True)))
+        ds3 = cat(parts, 1).astype(BF16)
+        dv = pick(tn(cat([a3.astype(BF16), t_ref[p]], 0), cat([ddh[p], doh[p]], 0)))
+        full = nt(spread(nn(flip, doh[p]).astype(BF16)), v)
+        for j in range(2):
+            m = jnp.where(near, full[j * rows:(j + 1) * rows], 0.0)
+            m = pltpu.roll(m, half + 1, 1, stride=1, stride_axis=0)
+            head = 2 * p + j
+            line, lane = at + 2 + head // per_row, head % per_row * rows
+            small_ref[line:line + 1, lane:lane + rows] = jnp.sum(m, axis=0, keepdims=True)
+        dkl = pick(tn(cat([ds1, ds2], 0), cat([q, ql], 0)))
+        dql = nn(cat([ds2, ds3], 1), cat([kld, kd], 0))
+        dqlh, dqll = split(dql)
+        dklh, dkll = split(dkl)
+        dq = nn(ds1, kld) + (tn(pool, dqlh) + tn(pool, dqll))
+        dk = pick(tn(ds3, ql)) + (tn(pool, dklh) + tn(pool, dkll))
+        for i, m in enumerate((dq * scale, dk * scale, dv)):
+            low = (m * valid).astype(BF16)
+            dqkv_ref[:, pl.ds(i * width + p * PAIR, PAIR)] = low
+    for i, line in ((0, at), (2, at + 1)):
+        small_ref[line:line + 1, :] = jnp.sum(
+            dqkv_ref[:, i * width:(i + 1) * width].astype(F32), axis=0, keepdims=True)
+    hook(3)
+    total = gr_ref[...]
+    for i in range(3):
+        total = total + nt(dqkv_ref[:, i * width:(i + 1) * width], stream.take(first_group + i))
+        stream.release(first_group + i)
+    gi_ref[...] = total.astype(BF16)
+    hook(4)
+
+
+def post_backward(
+    length, g, kept, vec_ref, gd_ref, gu_ref, gp_ref, gr_ref, do_ref, sums_ref, stream,
+    first_group, hook):
+    hat1_ref, hat2_ref, rstd_ref, slope_ref = kept
+    rows, width = hat1_ref.shape
+    chunks = gu_ref.shape[1] // width
+    row = lambda i: vec_ref[i:i + 1, :]
+
+    def total(i, values):
+        sums_ref[i:i + 1, :] = jnp.sum(values, axis=0, keepdims=True)
+
+    valid = lax.broadcasted_iota(jnp.int32, (rows, width), 0) < length
+    g = jnp.where(valid, g.astype(F32), 0.0)
+    hat2 = hat2_ref[...]
+    total(8, g * hat2)
+    total(9, g)
+    second = norm_back(g * row(8), hat2, rstd_ref[:, 1:2])
+    gd = second.astype(BF16)
+    gd_ref[...] = gd
+    total(7, gd.astype(F32))
+    grad = second
+    for c in range(chunks):
+        lanes = slice(c * width, (c + 1) * width)
+        gu = (nt(gd, stream.take(first_group + 2 * c)) * slope_ref[:, lanes]).astype(BF16)
+        stream.release(first_group + 2 * c)
+        gu_ref[:, lanes] = gu
+        total(3 + c, gu.astype(F32))
+        grad = grad + nt(gu, stream.take(first_group + 2 * c + 1))
+        stream.release(first_group + 2 * c + 1)
+    hat1 = hat1_ref[...]
+    total(1, grad * hat1)
+    total(2, grad)
+    residual = norm_back(grad * row(1), hat1, rstd_ref[:, 0:1])
+    gr_ref[...] = residual
+    gp = residual.astype(BF16)
+    gp_ref[...] = gp
+    total(0, gp.astype(F32))
+    do_ref[...] = nt(gp, stream.take(first_group + 2 * chunks))
+    stream.release(first_group + 2 * chunks)
+    hook()
+
+
+def post_groups(layer, chunks):
+    groups = []
+    for c in range(chunks):
+        groups += [(layer, 3, c, 0), (layer, 2, 0, c)]
+    return groups + [(layer, 1, 0, 0)]
+
+
+def post_backward_alone(
+    length_ref, g_ref, hat1_ref, hat2_ref, rstd_ref, slope_ref, vec_ref, *refs, layer):
+    own, other = (None,) + refs[:3], (None,) + refs[3:6]
+    gd_ref, gu_ref, gp_ref, gr_ref, do_ref, sums_ref, ring, sem = refs[6:]
+    chunks = gu_ref.shape[1] // g_ref.shape[1]
+    groups = post_groups(layer, chunks)
+    stream = Stream(groups, ring.shape[0], own, other, ring, sem)
+    stream.begin()
+    post_backward(length_ref[0], g_ref[...], (hat1_ref, hat2_ref, rstd_ref, slope_ref), vec_ref,
+                  gd_ref, gu_ref, gp_ref, gr_ref, do_ref, sums_ref, stream, 0, lambda: None)
+
+
+def greet_all(bits, near):
     barrier = pltpu.get_barrier_semaphore()
-    mine = lax.axis_index("section") == owner
-
-    @pl.when(mine)
-    def _():
-        pl.semaphore_signal(barrier, inc=1, device_id={"section": 1 - owner}, device_id_type=MESH)
-        for bit in range(bits):
-            pl.semaphore_signal(
-                barrier, inc=1, device_id={"batch": partner_of(bit)[0]}, device_id_type=MESH)
-        for bit in near:
-            pl.semaphore_signal(
-                barrier, inc=1, device_id={"section": 1 - owner, "batch": partner_of(bit)[0]},
-                device_id_type=MESH)
-        pl.semaphore_wait(barrier, bits)
-
-    @pl.when(jnp.logical_not(mine))
-    def _():
-        pl.semaphore_wait(barrier, 1 + len(near))
-
-
-def reduce_weights(*refs, weights, small):
-    count = len(weights)
-    owner, bits = small.owner, small.bits
-    xs, ys, vec = refs[:count], refs[count:2 * count], refs[2 * count]
-    outs, vec_out = refs[2 * count + 1:3 * count + 1], refs[3 * count + 1]
-    rest = refs[3 * count + 2:]
-    items = [w.bind(xs[i], ys[i], outs[i], rest[8 * i:8 * i + 8]) for i, w in enumerate(weights)]
-    items = [small.bind(vec, vec_out, rest[8 * count:])] + items
-    mine = lax.axis_index("section") == owner
-    greet(owner, bits, sorted({w.order[0] for w in weights}))
-
-    @pl.when(mine)
-    def _():
-        for item in items:
-            item.send_from_owner()
-        for item in items:
-            item.multiply()
-        for stage in range(bits):
-            for item in items:
-                if stage < item.stages:
-                    item.advance(stage)
-        for item in items:
-            item.drain()
-
-    @pl.when(jnp.logical_not(mine))
-    def _():
-        for item in items:
-            item.send_from_other()
-        for item in items:
-            item.sent_from_other()
+    other = 1 - lax.axis_index("section")
+    targets = [{"section": other}]
+    targets += [{"batch": partner_of(bit)[0]} for bit in range(bits)]
+    targets += [{"section": other, "batch": partner_of(bit)[0]} for bit in near]
+    for target in targets:
+        pl.semaphore_signal(barrier, inc=1, device_id=target, device_id_type=MESH)
+    pl.semaphore_wait(barrier, len(targets))
+
+
+class Take:
+    def __init__(self, refs):
+        self.refs, self.at = refs, 0
+
+    def __call__(self, count):
+        self.at += count
+        return self.refs[self.at - count:self.at]
+
+
+def backward(*refs, plans, littles, taps):
+    take = Take(refs)
+    (length_ref,) = take(1)
+    do2, gr2, sums2 = take(3)
+    factors2 = take(7)
+    factors1 = take(4)
+    kept2, kept1 = take(7), take(7)
+    newton2, newton1 = take(2)
+    errs = take(2)
+    post1, (vec1,) = take(4), take(1)
+    own, other = take(4), take(4)
+    count = len(plans[0])
+    outs = take(count)
+    small_out, ig_ref = take(2)
+    ring, ring_sem, newton_ref, newton_sem, gi_ref, gi_send, gi_recv = take(7)
+    dqkv2, gd1, gu1, gp1, dqkv1, gr1, do1 = take(7)
+    work, smalls = take(3), take(2)
+    weight_scratch = [take(8) for _ in range(count)]
+    small_scratch = take(4)
+    length = length_ref[0]
+    section = lax.axis_index("section")
+    rows, width = do2.shape
+    chunks = gu1.shape[1] // width
+    at = 6 + chunks
+    x2, y2 = factors2[:4], (factors2[4], factors2[5], dqkv2, factors2[6])
+    x1, y1 = factors1, (gd1, gu1, dqkv1, gp1)
+    items = []
+    for layer, xs, ys in ((0, x1, y1), (1, x2, y2)):
+        items.append([w.bind(xs[i], ys[i], outs[i], weight_scratch[i])
+                      for i, w in enumerate(plans[layer])]
+                     + [littles[layer].bind(smalls[layer], small_out, small_scratch)])
+    early, late = (0, 1, 3), (2, 4)
+
+    def newton_load(source):
+        return pltpu.make_async_copy(source, newton_ref, newton_sem)
+
+    groups = [(1, 0, 0, i) for i in range(3)] + post_groups(0, chunks) + [(0, 0, 0, i) for i in range(3)]
+    stream = Stream(groups, ring.shape[0], own, other, ring, ring_sem)
+    stream.begin()
+    newton_load(newton2).start()
+    greet_all(littles[0].bits, sorted({w.order[0] for w in plans[0]}))
+
+    def on(layer, owner_steps, other_steps):
+        @pl.when(section == layer)
+        def _():
+            for item, name, args in owner_steps:
+                getattr(items[layer][item], name)(*args)
+
+        @pl.when(section != layer)
+        def _():
+            for item, name, args in other_steps:
+                getattr(items[layer][item], name)(*args)
+
+    def send(layer, which):
+        on(layer, [(i, "send_from_owner", ()) for i in which],
+           [(i, "send_from_other", ()) for i in which])
+
+    def step(layer, which, name, *args):
+        on(layer, [(i, name, args) for i in which if not args or args[0] < items[layer][i].stages], [])
+
+    def share_gradient(layer):
+        def copy():
+            return pltpu.make_async_remote_copy(
+                src_ref=gi_ref.at[layer], dst_ref=ig_ref.at[pl.ds((1 - layer) * rows, rows)],
+                send_sem=gi_send.at[layer], recv_sem=gi_recv.at[layer],
+                device_id={"section": layer}, device_id_type=MESH)
+
+        @pl.when(section == layer)
+        def _():
+            ig_ref[layer * rows:(layer + 1) * rows, :] = gi_ref[layer]
+
+        @pl.when(section != layer)
+        def _():
+            copy().start()
+        return copy
+
+    send(1, early)
+    smalls[0][...] = jnp.zeros(smalls[0].shape, F32)
+    smalls[1][...] = jnp.zeros(smalls[1].shape, F32)
+    smalls[1][:at, :] = sums2[...]
+    for layer in range(2):
+        for i in range(NEWTON):
+            smalls[layer][at + 4 + i:at + 5 + i, :] = errs[layer][i]
+
+    def hook2(slot):
+        if slot == 3:
+            send(1, late)
+            newton_load(newton1).start()
+            step(1, (3, 0, 1), "multiply")
+
+    def hook1(slot):
+        if slot == 1:
+            step(1, (3, 0, 1), "advance", 0)
+            step(1, (4,), "multiply")
+        if slot == 2:
+            step(1, (3, 0, 1), "advance", 1)
+            step(1, (2,), "multiply")
+            step(1, (4,), "advance", 0)
+        if slot == 3:
+            send(0, late)
+            step(0, (3, 0, 1), "multiply")
+            step(1, (3, 0, 1), "advance", 2)
+            step(1, (4,), "advance", 1)
+
+    attention_backward(
+        length, do2, gr2, kept2, newton_ref, newton_load(newton2), dqkv2, gi_ref.at[1], smalls[1],
+        at, work, stream, 0, hook2, taps)
+    shared2 = share_gradient(1)
+    post_backward(length, gi_ref[1], post1, vec1, gd1, gu1, gp1, gr1, do1, smalls[0], stream, 3,
+                  lambda: send(0, early))
+    attention_backward(
+        length, do1, gr1, kept1, newton_ref, newton_load(newton1), dqkv1, gi_ref.at[0], smalls[0],
+        at, work, stream, 3 + len(post_groups(0, chunks)), hook1, taps)
+    shared1 = share_gradient(0)
+    bits = littles[0].bits
+    step(1, (2,), "advance", 0)
+    step(0, (4,), "multiply")
+    step(0, (3, 0, 1), "advance", 0)
+    step(1, (4,), "advance", 2)
+    step(1, (0, 1, 3), "advance", 3)
+    step(0, (2,), "multiply")
+    for stage in range(1, bits):
+        step(0, (4,), "advance", stage - 1)
+        step(0, (3, 0, 1), "advance", stage)
+        step(1, (2,), "advance", stage)
+        step(0, (2,), "advance", stage - 1)
+    step(1, (4,), "advance", bits - 1)
+    step(0, (4,), "advance", bits - 1)
+    step(0, (2,), "advance", bits - 1)
+    for layer in range(2):
+        on(layer, [(i, "drain", ()) for i in range(count + 1)],
+           [(i, "sent_from_other", ()) for i in range(count + 1)])
+    for layer, copy in ((0, shared1), (1, shared2)):
+        @pl.when(section == layer)
+        def _():
+            copy().wait_recv()
+
+        @pl.when(section != layer)
+        def _():
+            copy().wait_send()
+
+
+def attention_backward_alone(
+    length_ref, do_ref, gr_ref, qkv_ref, lm_ref, a1_ref, a2_ref, a3_ref, t_ref, db_ref, newton_in,
+    own, other, dqkv_ref, gi_ref, small_ref, ring, ring_sem, newton_ref, newton_sem, dz_ref, dr_ref,
+    da_ref, *, layer, at, taps):
+    stream = Stream([(layer, 0, 0, i) for i in range(3)], ring.shape[0], (own,), (other,), ring, ring_sem)
+    stream.begin()
+    load = pltpu.make_async_copy(newton_in, newton_ref, newton_sem)
+    load.start()
+    small_ref[...] = jnp.zeros(small_ref.shape, F32)
+    attention_backward(
+        length_ref[0], do_ref, gr_ref, (qkv_ref, lm_ref, a1_ref, a2_ref, a3_ref, t_ref, db_ref),
+        newton_ref, load, dqkv_ref, gi_ref, small_ref, at, (dz_ref, dr_ref, da_ref), stream, 0,
+        lambda slot: None, taps)
 
 
 def shape(dims, kind=F32):
@@ -772,7 +940,7 @@
         [IN_SMEM] + [IN_VMEM] * 3 + [ANYWHERE] * 2,
         [shape((rows, width), BF16), shape((3, rows, width), BF16), shape((2, LM, width), BF16),
          shape((rows, width)), shape((LM, width)), shape((LM, heads * rows)),
-         shape((pairs, rows, 2 * rows)), shape((4, NEWTON + 1, LM, width)),
+         shape((pairs, rows, 2 * rows), BF16), shape((4, NEWTON + 1, LM, width)),
          shape((2, LM, width), BF16), shape((NEWTON, 1, width))],
         [pltpu.VMEM((width, 3 * width), BF16), pltpu.SemaphoreType.DMA((3,))],
         (sel, x, bias, taps_row, weights[0], others[0]), 10 ** 10, 10 ** 7)
@@ -785,45 +953,27 @@
         [pltpu.VMEM((width, width), BF16), pltpu.VMEM((width, hidden), BF16),
          pltpu.VMEM((hidden, width), BF16), pltpu.SemaphoreType.DMA((1 + 2 * chunks,))],
         (sel, attended, x, vec) + tuple(weights[1:]) + tuple(others[1:]), 2 * 10 ** 9, 10 ** 7)
-    kept = dict(x=x, attended=attended, attention=(qkv, lm, a1, a2, a3, band, newton, db),
-                first=first, act=act, post=(hat1, hat2, rstd, slope))
-    return y, err, kept
-
-
-def backward_layer(sel, grad, kept, weights, others, vec, taps):
+    kept = dict(x=x, attended=attended, attention=(qkv, lm, a1, a2, a3, band, db), newton=newton,
+                first=first, act=act, post=(hat1, hat2, rstd, slope), err=err)
+    return y, kept
+
+
+def ring_scratch(slots, width):
+    return [pltpu.VMEM((slots, width, width), BF16), pltpu.SemaphoreType.DMA((slots,))]
+
+
+def post_backward_call(layer, length, grad, kept, weights, others, vec):
     rows, width = grad.shape
     hidden = weights[2].shape[1]
     chunks = hidden // width
-    hat1, hat2, rstd, slope = kept["post"]
-    gd, gu, gp, residual, d_attended, sums = call(
-        post_backward, "post_backward",
+    return call(
+        functools.partial(post_backward_alone, layer=layer), "post_backward",
         [IN_SMEM] + [IN_VMEM] * 6 + [ANYWHERE] * 6,
         [shape((rows, width), BF16), shape((rows, hidden), BF16), shape((rows, width), BF16),
          shape((rows, width)), shape((rows, width)), shape((4 + 2 + chunks, width))],
-        [pltpu.VMEM((width, width), BF16), pltpu.VMEM((width, hidden), BF16),
-         pltpu.VMEM((hidden, width), BF16), pltpu.SemaphoreType.DMA((1 + 2 * chunks,))],
-        (sel, grad, hat1, hat2, rstd, slope, vec) + tuple(weights[1:]) + tuple(others[1:]),
+        ring_scratch(9, width),
+        (length, grad) + kept["post"] + (vec,) + tuple(weights[1:]) + tuple(others[1:]),
         2 * 10 ** 9, 10 ** 7)
-    heads = width // LM
-    dqkv, gi, cols, dtaps = call(
-        functools.partial(attention_backward, taps=taps), "attention_backward",
-        [IN_SMEM] + [IN_VMEM] * 10 + [ANYWHERE] * 2,
-        [shape((rows, 3 * width), BF16), shape((rows, width), BF16), shape((3, width)),
-         shape((16, rows))],
-        [pltpu.VMEM((3, width, width), BF16), pltpu.VMEM((LM, width), F32),
-         pltpu.VMEM((LM, width), F32), pltpu.VMEM((LM, width), F32), pltpu.SemaphoreType.DMA((3,))],
-        (sel, d_attended, residual) + kept["attention"] + (weights[0], others[0]),
-        10 ** 10, 10 ** 7)
-    xs = (kept["act"], kept["first"], kept["x"], kept["attended"])
-    ys = (gd, gu, dqkv, gp)
-    return gi, xs, ys, sums, cols, dtaps[:heads]
-
-
-def small_rows(sums, cols, dtaps, err, width):
-    residuals = jnp.pad(jnp.sum(err, axis=(1, 2)), (0, width - NEWTON))
-    return jnp.concatenate([
-        sums, cols[0:1], cols[2:3], dtaps.reshape(-1, width), residuals[None],
-        jnp.zeros((16 - sums.shape[0] - 3 - dtaps.size // width, width), F32)], axis=0)
 
 
 def plan(owner, bits):
@@ -832,16 +982,78 @@
             Weight(owner, (1, 0, 2) + tail, False), Weight(owner, (2, 1, 0) + tail, False)]
 
 
-def reduce_on_slice(owner, xs, ys, small, batch):
+def small_shape(width, hidden, heads):
+    rows = 6 + hidden // width + 2 + heads * 128 // width + NEWTON
+    return (rows + 7) // 8 * 8, width
+
+
+def backward_on_slice(length, post2, kept, weights, others, vec, batch, taps):
+    gd, gu, gp, residual, d_attended, sums = post2
     bits = batch.bit_length() - 1
-    weights = [w.sizes(x.shape, y.shape) for w, x, y in zip(plan(owner, bits), xs, ys)]
-    outs = [shape((w.block, w.width)) for w in weights] + [shape(small.shape)]
-    little = Small(owner, bits)
-    scratch = [s for w in weights for s in w.scratch()] + little.scratch(small.shape)
+    rows, width = d_attended.shape
+    hidden, heads = gu.shape[1], width // LM
+    plans, littles = [], []
+    for layer in range(2):
+        xs = [kept[layer][n].shape for n in ("act", "first", "x", "attended")]
+        ys = [(rows, n) for n in (width, hidden, 3 * width, width)]
+        plans.append([w.sizes(a, b) for w, a, b in zip(plan(layer, bits), xs, ys)])
+        littles.append(Small(layer, bits))
+    dims = small_shape(width, hidden, heads)
+    factors = lambda k: tuple(k[n] for n in ("act", "first", "x", "attended"))
+    args = ((length, d_attended, residual, sums) + factors(kept[1]) + (gd, gu, gp)
+            + factors(kept[0]) + kept[1]["attention"] + kept[0]["attention"]
+            + (kept[1]["newton"], kept[0]["newton"], kept[0]["err"], kept[1]["err"])
+            + kept[0]["post"] + (vec,) + tuple(weights) + tuple(others))
+    ins = ([IN_SMEM] + [IN_VMEM] * 28 + [ANYWHERE] * 2 + [IN_VMEM] * 7 + [ANYWHERE] * 8)
+    outs = [shape((w.block, w.width)) for w in plans[0]] + [shape(dims), shape((2 * rows, width), BF16)]
+    dma = pltpu.SemaphoreType.DMA
+    low = lambda n: pltpu.VMEM((rows, n), BF16)
+    wide = lambda n: pltpu.VMEM((rows, n), F32)
+    scratch = ring_scratch(6, width) + [
+        pltpu.VMEM(kept[0]["newton"].shape, F32), dma(()), pltpu.VMEM((2, rows, width), BF16),
+        dma((2,)), dma((2,)), low(3 * width), low(width), low(hidden), low(width), low(3 * width),
+        wide(width), wide(width)]
+    scratch += [pltpu.VMEM((LM, width), F32)] * 3 + [pltpu.VMEM(dims, F32)] * 2
+    scratch += [s for w in plans[0] for s in w.scratch()] + littles[0].scratch(dims)
     return call(
-        functools.partial(reduce_weights, weights=weights, small=little),
-        "reduce_weights", [IN_VMEM] * (2 * len(xs) + 1), outs, scratch,
-        tuple(xs) + tuple(ys) + (small,), 4 * 10 ** 9, 10 ** 7, collective=owner)
+        functools.partial(backward, plans=plans, littles=littles, taps=taps), "backward",
+        ins, outs, scratch, args, 3 * 10 ** 10, 5 * 10 ** 7, collective=0)
+
+
+def backward_apart(length, post2, kept, weights, others, vecs, taps):
+    post, grads, shares = post2, [None, None], [None, None]
+    grad = None
+    for layer in (1, 0):
+        if layer == 0:
+            post = post_backward_call(0, length, grads[1], kept[0], weights, others, vecs[0])
+        gd, gu, gp, residual, d_attended, sums = post
+        rows, width = d_attended.shape
+        hidden = gu.shape[1]
+        dims = small_shape(width, hidden, width // LM)
+        at = sums.shape[0]
+        dqkv, grads[layer], small = call(
+            functools.partial(attention_backward_alone, layer=layer, at=at, taps=taps),
+            "attention_backward", [IN_SMEM] + [IN_VMEM] * 9 + [ANYWHERE] * 3,
+            [shape((rows, 3 * width), BF16), shape((rows, width), BF16), shape(dims)],
+            ring_scratch(3, width) + [pltpu.VMEM(kept[layer]["newton"].shape, F32),
+                                      pltpu.SemaphoreType.DMA(())]
+            + [pltpu.VMEM((LM, width), F32)] * 3,
+            (length, d_attended, residual) + kept[layer]["attention"]
+            + (kept[layer]["newton"], weights[0], others[0]), 10 ** 10, 10 ** 7)
+        errs = kept[layer]["err"].reshape(NEWTON, width)
+        end = at + 2 + width // LM * 128 // width
+        small = small.at[:at].set(sums).at[end:end + NEWTON].set(errs)
+        xs = [kept[layer][n] for n in ("act", "first", "x", "attended")]
+        products = [lax.dot_general(x, y, (((0,), (0,)), ((), ())), preferred_element_type=F32)
+                    for x, y in zip(xs, (gd, gu, dqkv, gp))]
+        shares[layer] = [
+            lax.psum_scatter(lax.psum(p, "section"), "batch", scatter_dimension=0, tiled=True)
+            for p in products] + [lax.psum(small, ("section", "batch"))]
+    lead = lax.axis_index("section") == 0
+    crossed = swap(jnp.where(lead, grads[1], grads[0]))
+    together = jnp.where(
+        lead, jnp.concatenate([grads[0], crossed]), jnp.concatenate([crossed, grads[1]]))
+    return [jnp.where(lead, a, b) for a, b in zip(*shares)] + [together]
 
 
 def swap(value):
@@ -866,7 +1078,6 @@
               tap_rows.reshape(-1, width)]
     vec = jnp.concatenate(pieces, axis=0)
     vec_other = swap(vec)
-    count = seq_lengths.shape[0]
     length = lax.dynamic_index_in_dim(seq_lengths, section, keepdims=False)
     own_rows = lambda v: lax.dynamic_slice_in_dim(v, section * rows, rows, 0)
     sels, vecs, biases, tap_list = [], [], [], []
@@ -879,29 +1090,23 @@
         t = v[12:].reshape(heads, 128)
         tap_list.append(jnp.pad(t, ((0, 16 - heads), (0, 0))))
     value = own_rows(layer_input)
-    outputs, residuals, kept = [], [], []
+    outputs, kept = [], []
     for layer in range(2):
-        value, err, saved = forward_layer(
+        value, saved = forward_layer(
             sels[layer], value, weights, others, vecs[layer], biases[layer], tap_list[layer], taps)
         outputs.append(value)
-        residuals.append(err)
         kept.append(saved)
     crossed = swap(jnp.where(lead, outputs[1], outputs[0]))
     activations = jnp.where(
         lead, jnp.concatenate([outputs[0], crossed]), jnp.concatenate([crossed, outputs[1]]))
-    grad = own_rows(cotangent)
-    shares, grads = [None, None], [None, None]
-    for layer in (1, 0):
-        grad, xs, ys, sums, cols, dtaps = backward_layer(
-            sels[layer], grad, kept[layer], weights, others, vecs[layer], taps)
-        grads[layer] = grad
-        small = small_rows(sums, cols, dtaps, residuals[layer], width)
-        shares[layer] = reduce_layer(layer, xs, ys, small, batch)
-    crossed = swap(jnp.where(lead, grads[1], grads[0]))
-    input_grads = jnp.where(
-        lead, jnp.concatenate([grads[0], crossed]), jnp.concatenate([crossed, grads[1]]))
-    g_red, g_exp, g_qkv, g_out, small = [
-        jnp.where(lead, a, b) for a, b in zip(shares[0], shares[1])]
+    length = length[None]
+    post2 = post_backward_call(1, length, own_rows(cotangent), kept[1], weights, others, vecs[1])
+    blocks = [w.shape[0] // batch for w in weights]
+    if batch >= 8 and all(b % 16 == 0 for b in blocks):
+        result = backward_on_slice(length, post2, kept, weights, others, vecs[0], batch, taps)
+    else:
+        result = backward_apart(length, post2, kept, weights, others, vecs, taps)
+    g_red, g_exp, g_qkv, g_out, small, input_grads = result
     index = lax.axis_index("batch")
 
     def share(first, many):
@@ -911,21 +1116,13 @@
 
     chunks = reduce_weight.shape[1] // width
     at = 6 + chunks
-    dtaps = small[at + 2:at + 2 + heads * 128 // width].reshape(heads, 128)[:, :taps]
-    proxies = small[at + 2 + heads * 128 // width, :NEWTON]
+    end = at + 2 + heads * 128 // width
+    dtaps = small[at + 2:end].reshape(heads, 128)[:, :taps]
+    proxies = jnp.sum(small[end:end + NEWTON], axis=1)
     return (
         activations[None], input_grads[None], g_qkv[None], share(at, 2), dtaps[None], g_out[None],
         share(0, 1), share(1, 1), share(2, 1), g_exp[None], share(3, chunks), g_red[None],
         share(3 + chunks, 1), share(4 + chunks, 1), share(5 + chunks, 1), proxies[None])
-
-
-def reduce_layer(layer, xs, ys, small, batch):
-    if all((x.shape[1] // batch) % 16 == 0 for x in xs) and batch >= 8:
-        return reduce_on_slice(layer, xs, ys, small, batch)
-    products = [lax.dot_general(x, y, (((0,), (0,)), ((), ())), preferred_element_type=F32)
-                for x, y in zip(xs, ys)]
-    return [lax.psum_scatter(lax.psum(p, "section"), "batch", scatter_dimension=0, tiled=True)
-            for p in products] + [lax.psum(small, ("section", "batch"))]
 
 
 def solution(mesh):

time: 325 us -> 270 us (0.83)
  Pallas kernels: 267 us -> 223 us
  other arithmetic: 13.7 us -> 6.32 us
  local copies, waits for them, and re-layouts: 27.9 us -> 24.4 us
    pallas_call x10 -> x6, Pallas kernels: 267 us -> 223 us  [call(): pl.pallas_call(kernel, out_shape=tuple(outs), in_specs=ins, out_specs=(IN...]
    unnamed x38 -> x21, local copies, waits for them, and re-layouts: 2.27 us -> 10.1 us
    broadcast_in_dim x4 -> x0, other arithmetic: 5.4 us -> none  [the longest x1 1.96 us: body(): g_red[None]]
    dynamic_slice x7, local copies, waits for them, and re-layouts: 8.2 us -> 4.13 us  [share(): return lax.dynamic_slice_in_dim(flat, index * size, size, 0)[None]]
    concatenate x2 -> x0, local copies, waits for them, and re-layouts: 3.99 us -> none  [small_rows(): jnp.concatenate([sums, cols[0:1], cols[2:3], dtaps.reshape(-1, width), re...]
    ppermute x7 -> x6, waiting for transfers between devices: 8.8 us -> 8.67 us  [swap(): return lax.ppermute(value, 'section', [(0, 1), (1, 0)])]
  transfers between devices with their start and end apart: 7 -> 6, of which waited for: 1 -> 1; matrix products, arithmetic and copies ran while one was open for 7% -> 5% of each run, Pallas kernels for 7% -> 9%
where the time goes in v3:
time: 270 us; the launch traced here: 266 us
  Pallas kernels  223 us (83%)
  local copies, waits for them, and re-layouts  24.4 us (9%)
  waiting for transfers between devices  8.67 us (3%)
  other arithmetic  6.32 us (2%)
    pallas_call x6, Pallas kernels, call(): pl.pallas_call(kernel, out_shape=tuple(outs), in_specs=ins, out_specs=(IN...  223 us
    unnamed x21, local copies, waits for them, and re-layouts  10.1 us
    ppermute x6, waiting for transfers between devices, swap(): return lax.ppermute(value, 'section', [(0, 1), (1, 0)])  8.67 us
  transfers between devices with their start and end apart: 6, of which 1 were waited for; matrix products, arithmetic and copies ran while one was open for 5% of the time, Pallas kernels for 9%

profile of v3, /device:TPU:0, one launch (start us, length us, event | category | flops | bytes accessed | tf_op | source)
XLA Modules:
  0.0 265.5 jit_solution(844795778657425718)
XLA Ops:
  2.2 1.4 reduce.4
  4.3 0.7 reduce.1
  5.0 1.5 concatenate.29
  7.1 1.2 dynamic_slice.34.length_ref.refs_0_
  9.0 1.6 constant_dynamic-slice_fusion.6.g_ref
  10.7 1.2 pad_add_fusion
  14.0 8.7 %collective-permute-done.1.other_ref.refs_42_ = bf16[768,2304]{1,0:T(8,128)(2,1)} collective-permute-done((bf16[768,2304]{1,0:T(8,128)(2,1)}, bf16[768,2304]{1,0:T(8,128)(2,1)}, u32[]{:S(2)}, u32[]{:S(2)}) %collective-permute-start.1) | collective-permute-done | bytes 3538976 | tf_op jit(solution)/shard_map/ppermute | solution.py:1060
  22.6 23.7 %attention_forward.2 = (bf16[128,768]{1,0:T(8,128)(2,1)}, bf16[3,128,768]{2,1,0:T(8,128)(2,1)}, bf16[2,64,768]{2,1,0:T(8,128)(2,1)}, f32[128,768]{1,0:T(8,128)},...) custom-call(s32[2]{0:T(128)} %get-tuple-element.124.sel_ref, ...), custom_call_target="tpu_custom_call" | custom-call | flops 10000000000 | bytes 10000000 | tf_op jit(solution)/shard_map/attention_forward/pallas_call | solution.py:927
  46.4 1.0 copy-done.1
  47.4 7.3 %post_forward.2 = (bf16[128,768]{1,0:T(8,128)(2,1)}, bf16[128,768]{1,0:T(8,128)(2,1)}, bf16[128,3072]{1,0:T(8,128)(2,1)}, f32[128,768]{1,0:T(8,128)}, f32[128,76...) custom-call(s32[2]{0:T(128)} %get-tuple-element.124.sel_ref, ...), custom_call_target="tpu_custom_call" | custom-call | flops 2000000000 | bytes 10000000 | tf_op jit(solution)/shard_map/post_forward/pallas_call | solution.py:927
  54.7 23.7 %attention_forward.3 = (bf16[128,768]{1,0:T(8,128)(2,1)}, bf16[3,128,768]{2,1,0:T(8,128)(2,1)}, bf16[2,64,768]{2,1,0:T(8,128)(2,1)}, f32[128,768]{1,0:T(8,128)},...) custom-call(s32[2]{0:T(128)} %get-tuple-element.125.sel_ref, ...), custom_call_target="tpu_custom_call" | custom-call | flops 10000000000 | bytes 10000000 | tf_op jit(solution)/shard_map/attention_forward/pallas_call | solution.py:927
  78.4 7.4 %post_forward.3 = (bf16[128,768]{1,0:T(8,128)(2,1)}, bf16[128,768]{1,0:T(8,128)(2,1)}, bf16[128,3072]{1,0:T(8,128)(2,1)}, f32[128,768]{1,0:T(8,128)}, f32[128,76...) custom-call(s32[2]{0:T(128)} %get-tuple-element.125.sel_ref, ...), custom_call_target="tpu_custom_call" | custom-call | flops 2000000000 | bytes 10000000 | tf_op jit(solution)/shard_map/post_forward/pallas_call | solution.py:927
  85.8 9.7 %post_backward.1 = (bf16[128,768]{1,0:T(8,128)(2,1)}, bf16[128,3072]{1,0:T(8,128)(2,1)}, bf16[128,768]{1,0:T(8,128)(2,1)}, f32[128,768]{1,0:T(8,128)}, f32[128,768]{1,0:T(8,128)}, /*index=5*/f32[10,768]{1,0:T(8,128)}) custom-call(s32[1]{0:T(128)} %dynamic_slice.34.length_ref.refs_0_, bf16[128,768]{1,0:T(8,128)(2,1)} %constant_dynamic-slice_fusion.6.g_ref, ...), custom_call_target="tpu_custom_call" | custom-call | flops 2000000000 | bytes 10000000 | tf_op jit(solution)/shard_map/post_backward/pallas_call | solution.py:927
  95.5 151.7 %backward.1 = (f32[192,768]{1,0:T(8,128)}, f32[48,3072]{1,0:T(8,128)}, f32[48,2304]{1,0:T(8,128)}, f32[48,768]{1,0:T(8,128)}, f32[24,768]{1,0:T(8,128)}, /*index=5*/bf16[256,768]{1,0:T(8,128)(2,1)}) custom-call(s32[1]{0:T(128)} %dynamic_slice.34.length_ref.refs_0_, f32[128,768]{1,0:T(8,128)} %get-tuple-element.70.refs_1_, ...), custom_call_target="tpu_custom_call" | custom-call | flops 30000001024 | bytes 50000000 | tf_op jit(solution)/shard_map/backward/pallas_call | solution.py:927
  247.2 0.8 slice.63
  248.0 0.8 fusion.1
  248.8 0.9 fusion
  255.2 1.4 slice_reduce_fusion
  256.6 0.8 maximum_select_fusion
  257.5 1.8 copy.40
  259.2 1.8 copy.41
  261.0 1.6 copy.42
  262.6 1.9 copy.43
  264.5 0.8 copy.44
  (54 shorter events, 11.0 us)
Async XLA Ops:
  0.6 7.7 %copy-start = (bf16[256,768]{1,0:T(8,128)(2,1)S(1)}, bf16[256,768]{1,0:T(8,128)(2,1)}, u32[]{:S(2)}) copy-start(bf16[256,768]{1,0:T(8,128)(2,1)} %param.16) | copy-start | bytes 1179652
  0.7 45.7 %collective-permute-start.3 = (bf16[768,3072]{1,0:T(8,128)(2,1)}, bf16[768,3072]{1,0:T(8,128)(2,1)}, u32[]{:S(2)}, u32[]{:S(2)}) collective-permute-start(bf16[768,3072]{1,0:T(8,128)(2,1)} %bitcast.23), channel_id=1, source_target_pairs={{0,16},{16,0},{1,17},{17,1},{2,18},{18,2},{3,19},{19,3},{4,20},{20... | collective-permute-start | bytes 14155784 | tf_op jit(solution)/shard_map/ppermute | solution.py:1060
  1.2 45.2 %collective-permute-start.4 = (bf16[3072,768]{1,0:T(8,128)(2,1)}, bf16[3072,768]{1,0:T(8,128)(2,1)}, u32[]{:S(2)}, u32[]{:S(2)}) collective-permute-start(bf16[3072,768]{1,0:T(8,128)(2,1)} %bitcast.28), channel_id=1, source_target_pairs={{0,16},{16,0},{1,17},{17,1},{2,18},{18,2},{3,19},{19,3},{4,20},{20... | collective-permute-start | bytes 14155784 | tf_op jit(solution)/shard_map/ppermute | solution.py:1060
  1.3 21.4 %collective-permute-start.1 = (bf16[768,2304]{1,0:T(8,128)(2,1)}, bf16[768,2304]{1,0:T(8,128)(2,1)}, u32[]{:S(2)}, u32[]{:S(2)}) collective-permute-start(bf16[768,2304]{1,0:T(8,128)(2,1)} %bitcast.50), channel_id=1, source_target_pairs={{0,16},{16,0},{1,17},{17,1},{2,18},{18,2},{3,19},{19,3},{4,20},{20... | collective-permute-start | bytes 10616840 | tf_op jit(solution)/shard_map/ppermute | solution.py:1060
  6.5 5.4 %collective-permute-start = (f32[14,768]{1,0:T(8,128)S(1)}, f32[14,768]{1,0:T(8,128)S(1)}, u32[]{:S(2)}, u32[]{:S(2)}) collective-permute-start(f32[14,768]{1,0:T(8,128)S(1)} %concatenate.29), channel_id=1, source_target_pairs={{0,16},{16,0},{1,17},{17,1},{2,18},{18,2},{3,19},{19,3},{4,20},{20... | collective-permute-start | bytes 129032 | tf_op jit(solution)/shard_map/ppermute | solution.py:1060
  6.7 39.6 %collective-permute-start.2 = (bf16[768,768]{1,0:T(8,128)(2,1)}, bf16[768,768]{1,0:T(8,128)(2,1)S(1)}, u32[]{:S(2)}, u32[]{:S(2)}) collective-permute-start(bf16[768,768]{1,0:T(8,128)(2,1)} %bitcast.33), channel_id=1, source_target_pairs={{0,16},{16,0},{1,17},{17,1},{2,18},{18,2},{3,19},{19,3},{4,20},{20... | collective-permute-start | bytes 3538952 | tf_op jit(solution)/shard_map/ppermute | solution.py:1060
  12.0 34.3 %copy-start.5 = (f32[14,768]{1,0:T(8,128)}, f32[14,768]{1,0:T(8,128)S(1)}, u32[]{:S(2)}) copy-start(f32[14,768]{1,0:T(8,128)S(1)} %get-tuple-element.108.vec_ref) | copy-start | bytes 129028
  12.0 34.3 %copy-start.6 = (f32[14,768]{1,0:T(8,128)}, f32[14,768]{1,0:T(8,128)S(1)}, u32[]{:S(2)}) copy-start(f32[14,768]{1,0:T(8,128)S(1)} %get-tuple-element.109.vec_ref.refs_37_) | copy-start | bytes 129028
  46.3 1.0 copy-start.1
  95.5 158.4 %copy-start.2 = (bf16[128,768]{1,0:T(8,128)(2,1)S(1)}, bf16[128,768]{1,0:T(8,128)(2,1)}, u32[]{:S(2)}) copy-start(bf16[128,768]{1,0:T(8,128)(2,1)} %get-tuple-element.63.x_ref.refs_6_) | copy-start | bytes 589828
  95.5 158.4 %copy-start.3 = (bf16[128,768]{1,0:T(8,128)(2,1)S(1)}, bf16[128,768]{1,0:T(8,128)(2,1)}, u32[]{:S(2)}) copy-start(bf16[128,768]{1,0:T(8,128)(2,1)} %get-tuple-element.65) | copy-start | bytes 589828
  247.2 17.3 %copy-start.4 = (f32[192,768]{1,0:T(8,128)S(1)}, f32[192,768]{1,0:T(8,128)}, u32[]{:S(2)}) copy-start(f32[192,768]{1,0:T(8,128)} %get-tuple-element.107) | copy-start | bytes 1769476
  253.9 2.7 %collective-permute-start.5 = (bf16[128,768]{1,0:T(8,128)(2,1)S(1)}, bf16[128,768]{1,0:T(8,128)(2,1)S(1)}, u32[]{:S(2)}, u32[]{:S(2)}) collective-permute-start(bf16[128,768]{1,0:T(8,128)(2,1)S(1)} %broadcast_select_fusion), channel_id=1, source_target_pairs={{0,16},{16,0},{1,17},{17,1},{2,18},{18,2},{3,19},{19,3},{4,20},{20... | collective-permute-start | bytes 589832 | tf_op jit(solution)/shard_map/ppermute | solution.py:1060
